TPU v7x, 512 devices: a whole 4x8x8 slice. The times are simulated.
512 devices in a mesh: rows: 8 (over z), cx: 8 (over y), cy: 8 (over x, core).
Axes of the slice: x: 4, y: 8, z: 8, core: 2. Of those that a mesh axis runs over, the one named last changes fastest.
Arguments:
- rows_data: float32 [32768, 1024], P(('rows', 'cx', 'cy')), may hold values from -6 to 6
- owner_rows: int32 [32768, 1], P(('rows', 'cx', 'cy')), may hold values from 0 to 63; in each aligned block of 64 rows (0 to 63, 64 to 127, ...) at most 2 rows name the same one
- slot_rows: int32 [32768], P(('rows', 'cx', 'cy')), may hold values from 0 to 2047
- centroids: float32 [131072, 1024], P(('cx', 'cy'), 'rows'), may hold values from -6 to 6
- counts: float32 [131072], P(('cx', 'cy')), may hold values from 1 to 100
- owner_cent: int32 [131072, 1], P(('cx', 'cy')), may hold values from 0 to 63; in each aligned block of 2048 rows (0 to 2047, 2048 to 4095, ...) at most 64 rows name the same one
- slot_cent: int32 [131072], P(('cx', 'cy')), may hold values from 0 to 63
- upper: float32 [4096, 1024], P(('cx', 'cy'), 'rows'), may hold values from -6 to 6
- upper_counts: float32 [4096], P(('cx', 'cy')), may hold values from 1 to 100
Outputs:
- moved: float32 [131072, 1024], P(('cx', 'cy'), 'rows')
- new_counts: float32 [131072], P(('cx', 'cy'))
- new_upper: float32 [4096, 1024], P(('cx', 'cy'), 'rows')
- new_upper_counts: float32 [4096], P(('cx', 'cy'))
Inputs may be any that keep to these rules, and one draw needn't show every extreme that they name: `owner_rows`: the rows of one device name each value at most 2 times, and some device reaches it. `owner_cent`: the 2048 level-1 centroids of one shard name each value at most 64 times, and some shard reaches it.
All inputs are finite; a program needn't handle non-finite values.
Results may differ from a plain program's by a relative error of at most 0.00002.
Values sent between devices are 32-bit elements; how exact they have to be, the bound alone decides.
No kernel may reach another device: no remote copies, remote signals or barrier semaphores. Data moves between devices by JAX's collectives and lax.ppermute only.
A program may use at most 64 MiB of HBM per device.

v0:
```python
import jax
import jax.numpy as jnp
from jax import lax
from jax.sharding import PartitionSpec as P


def in_blocks(x, dim, count):
    shape = x.shape
    parts = x.reshape(*shape[:dim], count, shape[dim] // count, *shape[dim + 1 :])
    return jnp.moveaxis(parts, dim, 0)


def laid_out(parts, dim):
    parts = jnp.moveaxis(parts, 0, dim)
    shape = parts.shape
    return parts.reshape(*shape[:dim], shape[dim] * shape[dim + 1], *shape[dim + 2 :])


def joined_exchange(x, axis, axes, splits, concats):
    sizes = [lax.axis_size(a) for a in axes]
    parts = in_blocks(x, splits[0], sizes[0])
    parts = jnp.moveaxis(in_blocks(parts, splits[1] + 1, sizes[1]), 0, 1)
    inside = parts.shape[2:]
    parts = parts.reshape(-1, *inside)
    parts = lax.all_to_all(parts, axis, split_axis=0, concat_axis=0, tiled=True)
    parts = laid_out(parts.reshape(*sizes, *inside), concats[0] + 1)
    return laid_out(parts, concats[1])


def sum_at_owner(x, axis, dim):
    count = lax.axis_size(axis)
    parts = lax.all_to_all(in_blocks(x, dim, count), axis, 0, 0, tiled=True)
    return jnp.sum(parts, axis=0)


def bucket(values, owners, slot_ids, shards, capacity, empty):
    onehot = (owners[:, None] == jnp.arange(shards, dtype=jnp.int32)[None, :]).astype(jnp.int32)
    earlier = jnp.cumsum(onehot, axis=0) - onehot
    position = jnp.sum(earlier * onehot, axis=1)
    target = owners * capacity + position
    buffer = jnp.zeros((shards * capacity, values.shape[1]), values.dtype).at[target].set(values)
    labels = jnp.full((shards * capacity,), empty, jnp.int32).at[target].set(slot_ids)
    return (buffer.reshape(shards, capacity, values.shape[1]), labels.reshape(shards, capacity))


def accumulate(values, labels, segments):
    summed = jnp.zeros((segments, values.shape[1]), jnp.float32).at[labels].add(values, mode="drop")
    member_counts = (
        jnp.zeros((segments,), jnp.float32)
        .at[labels]
        .add(jnp.ones(labels.shape, jnp.float32), mode="drop")
    )
    return (summed, member_counts)


def damped(previous, weights, summed, member_counts):
    denominator = weights + member_counts
    updated = previous + (summed - member_counts[:, None] * previous) / denominator[:, None]
    return (updated, denominator)


def body(
    rows_data, owner_rows, slot_rows, centroids, counts, owner_cent, slot_cent, upper, upper_counts
):
    shards = lax.axis_size(("cx", "cy"))
    groups = lax.axis_size("rows")
    batch = rows_data.shape[0]
    lower_rows = centroids.shape[0]
    capacity = 2 * batch // shards
    buffer, labels = bucket(rows_data, owner_rows[:, 0], slot_rows, shards, capacity, lower_rows)
    labels = jnp.broadcast_to(labels[:, :, None], (shards, capacity, groups))
    arrived, arrived_labels = (
        joined_exchange(buffer, ("rows", "cx", "cy"), ("rows", ("cx", "cy")), (2, 0), (1, 0)),
        joined_exchange(labels, ("rows", "cx", "cy"), ("rows", ("cx", "cy")), (2, 0), (1, 0)),
    )
    slice_width = arrived.shape[2]
    summed, member_counts = accumulate(
        arrived.reshape(-1, slice_width), arrived_labels.reshape(-1), lower_rows
    )
    moved, new_counts = damped(centroids, counts, summed, member_counts)
    upper_rows = upper.shape[0]
    owners_upper = owner_cent[:, 0]
    labels_upper = owners_upper * upper_rows + slot_cent
    whole_partial, hit_counts = accumulate(moved, labels_upper, upper_rows * shards)
    upper_summed = sum_at_owner(whole_partial, ("cx", "cy"), 0)
    upper_members = sum_at_owner(hit_counts, ("cx", "cy"), 0)
    new_upper, new_upper_counts = damped(upper, upper_counts, upper_summed, upper_members)
    return (moved, new_counts, new_upper, new_upper_counts)


def solution(mesh):
    placed = (
        P(("rows", "cx", "cy"), None),
        P(("rows", "cx", "cy"), None),
        P(("rows", "cx", "cy")),
        P(("cx", "cy"), "rows"),
        P(("cx", "cy")),
        P(("cx", "cy"), None),
        P(("cx", "cy")),
        P(("cx", "cy"), "rows"),
        P(("cx", "cy")),
    )
    return jax.shard_map(
        body,
        mesh=mesh,
        in_specs=placed,
        out_specs=(
            P(("cx", "cy"), "rows"),
            P(("cx", "cy")),
            P(("cx", "cy"), "rows"),
            P(("cx", "cy")),
        ),
        check_vma=False,
    )
```

profile of v0, /device:TPU:1, one launch (start us, length us, event | category | flops | bytes accessed | tf_op | source)
XLA Modules:
  0.0 163.1 jit_solution(14863680592584377363)
XLA Ops:
  0.6 0.7 fusion.6
  1.4 0.1 reduce_window_sum.11
  1.5 0.8 select_reduce_fusion
  2.3 0.7 fusion.11
  3.0 0.9 scatter_custom_fusion
  3.9 0.1 broadcast_in_dim.44
  4.0 0.7 transpose.21
  4.7 22.2 %all-to-all-start = ((s32[512,1,2,1]{2,3,1,0:T(1,128)}), s32[512,1,2,1]{2,3,1,0:T(1,128)S(1)}, u32[]{:S(2)}, u32[]{:S(2)}) async-start(s32[512,1,2,1]{2,3,1,0:T(1,128)} %bitcast.3), calls=%async_computation | async-start | bytes 524288 | tf_op jit(solution)/shard_map/all_to_all | solution.py:25
  26.9 1.4 scatter_custom_fusion.1
  28.3 0.0 copy-start.6
  28.3 0.0 copy-start.4
  28.3 0.1 copy.38
  28.4 0.0 copy-start.5
  28.4 0.2 copy.32
  28.6 1.2 copy.33
  29.8 14.6 %all-to-all-done = s32[512,1,2,1]{2,3,1,0:T(1,128)S(1)} async-done(((s32[512,1,2,1]{2,3,1,0:T(1,128)}), s32[512,1,2,1]{2,3,1,0:T(1,128)S(1)}, u32[]{:S(2)}, u32[]{:S(2)}) %all-to-all-start) | async-done | bytes 4128 | tf_op jit(solution)/shard_map/all_to_all | solution.py:25
  44.3 8.4 %all-to-all-start.1 = ((f32[512,1,2,128]{3,2,1,0:T(2,128)}), f32[512,1,2,128]{3,2,1,0:T(2,128)S(1)}, u32[]{:S(2)}, u32[]{:S(2)}) async-start(f32[512,1,2,128]{3,2,1,0:T(2,128)} %copy.33), calls=%async_computation.1 | async-start | bytes 1048576 | tf_op jit(solution)/shard_map/all_to_all | solution.py:25
  52.7 0.0 copy-done.6
  52.7 0.0 copy-start
  52.8 0.0 copy-done.4
  52.8 11.2 %scatter_custom_fusion.5 = f32[4096]{0:T(1024)S(1)} fusion(s32[2048]{0:T(1024)S(1)} %compare_select_fusion.1, f32[2048]{0:T(1024)S(1)} %broadcast.56, f32[]{:T(128)} %constant.8.clone.1), kind=kCustom, calls=%fused_computation.19 | custom fusion | flops 2048 | bytes 16388 | tf_op jit(solution)/shard_map/scatter-add | solution.py:51
  64.1 0.7 all_to_all.18
  64.8 0.1 copy.37
  64.9 0.2 copy.31
  65.1 0.2 reshape_reshape_reshape.6
  65.3 5.9 %scatter_custom_fusion.3 = f32[2048]{0:T(1024)S(1)} fusion(s32[1024]{0:T(1024)S(1)} %bitcast.39, f32[1024]{0:T(1024)S(1)} %broadcast.55, f32[]{:T(128)} %constant.8.clone.1), kind=kCustom, calls=%fused_computation.22 | custom fusion | flops 1024 | bytes 8196 | tf_op jit(solution)/shard_map/scatter-add | solution.py:51
  71.2 0.0 copy-done.5
  71.2 0.0 copy-start.2
  71.2 4.2 %all-to-all-done.1 = f32[512,1,2,128]{3,2,1,0:T(2,128)S(1)} async-done(((f32[512,1,2,128]{3,2,1,0:T(2,128)}), f32[512,1,2,128]{3,2,1,0:T(2,128)S(1)}, u32[]{:S(2)}, u32[]{:S(2)}) %all-to-all-start.1) | async-done | bytes 524320 | tf_op jit(solution)/shard_map/all_to_all | solution.py:25
  75.4 6.3 %all-to-all-start.3 = ((f32[64,1,64]{2,1,0:T(1,128)}), f32[64,1,64]{2,1,0:T(1,128)S(1)}, u32[]{:S(2)}, u32[]{:S(2)}) async-start(f32[64,1,64]{2,1,0:T(1,128)} %all_to_all.18), calls=%async_computation.3 | async-start | bytes 65536 | tf_op jit(solution)/shard_map/all_to_all | solution.py:32
  81.8 0.4 copy.35
  82.2 6.3 %scatter_custom_fusion.2 = f32[2048,128]{1,0:T(8,128)S(1)} fusion(s32[1024]{0:T(1024)S(1)} %bitcast.40, f32[1024,128]{1,0:T(8,128)S(1)} %bitcast.35, f32[]{:T(128)} %constant.8.clone.1), kind=kCustom, calls=%fused_computation.9 | custom fusion | flops 131072 | bytes 1048580 | tf_op jit(solution)/shard_map/scatter-add | solution.py:47
  88.5 0.0 copy-done
  88.5 0.7 divide_add_fusion
  89.2 0.0 copy-done.2
  89.2 0.0 copy-start.1
  89.2 12.9 %scatter_custom_fusion.4 = f32[4096,128]{1,0:T(8,128)} fusion(s32[2048]{0:T(1024)S(1)} %compare_select_fusion.1, f32[2048,128]{1,0:T(8,128)S(1)} %divide_add_fusion, f32[]{:T(128)} %constant.8.clone.1), kind=kCustom, calls=%fused_computation.6 | custom fusion | flops 262144 | bytes 2097156 | tf_op jit(solution)/shard_map/scatter-add | solution.py:47
  102.1 0.0 all-to-all-done.3
  102.1 0.0 copy-start.8
  102.1 0.0 copy-done.1
  102.1 10.4 %all-to-all-start.2 = ((f32[64,64,128]{2,1,0:T(8,128)}), f32[64,64,128]{2,1,0:T(8,128)S(1)}, u32[]{:S(2)}, u32[]{:S(2)}) async-start(f32[64,64,128]{2,1,0:T(8,128)} %bitcast.13), calls=%async_computation.2 | async-start | bytes 4194304 | tf_op jit(solution)/shard_map/all_to_all | solution.py:32
  112.6 0.0 copy-start.3
  112.6 0.0 copy-done.8
  112.6 0.0 copy-start.7
  112.7 49.6 %all-to-all-done.2 = f32[64,64,128]{2,1,0:T(8,128)S(1)} async-done(((f32[64,64,128]{2,1,0:T(8,128)}), f32[64,64,128]{2,1,0:T(8,128)S(1)}, u32[]{:S(2)}, u32[]{:S(2)}) %all-to-all-start.2) | async-done | bytes 2097184 | tf_op jit(solution)/shard_map/all_to_all | solution.py:32
  162.3 0.1 reduce_sum.31
  162.4 0.0 copy-done.3
  162.4 0.7 divide_add_fusion.1
  163.1 0.0 copy-done.7
  (9 shorter events, 0.1 us)
Async XLA Ops:
  4.7 39.6 %all-to-all-start = ((s32[512,1,2,1]{2,3,1,0:T(1,128)}), s32[512,1,2,1]{2,3,1,0:T(1,128)S(1)}, u32[]{:S(2)}, u32[]{:S(2)}) async-start(s32[512,1,2,1]{2,3,1,0:T(1,128)} %bitcast.3), calls=%async_computation | async-start | bytes 524288 | tf_op jit(solution)/shard_map/all_to_all | solution.py:25
  28.3 24.5 %copy-start.6 = (s32[2048,1]{0,1:T(1,128)S(1)}, s32[2048,1]{0,1:T(1,128)}, u32[]{:S(2)}) copy-start(s32[2048,1]{0,1:T(1,128)} %param.14) | copy-start | bytes 24580
  28.3 24.5 %copy-start.4 = (s32[2048]{0:T(1024)S(1)}, s32[2048]{0:T(1024)}, u32[]{:S(2)}) copy-start(s32[2048]{0:T(1024)} %param.15) | copy-start | bytes 24580
  28.4 42.8 %copy-start.5 = (f32[2048]{0:T(1024)S(1)}, f32[2048]{0:T(1024)}, u32[]{:S(2)}) copy-start(f32[2048]{0:T(1024)} %param.13) | copy-start | bytes 24580
  44.3 31.1 %all-to-all-start.1 = ((f32[512,1,2,128]{3,2,1,0:T(2,128)}), f32[512,1,2,128]{3,2,1,0:T(2,128)S(1)}, u32[]{:S(2)}, u32[]{:S(2)}) async-start(f32[512,1,2,128]{3,2,1,0:T(2,128)} %copy.33), calls=%async_computation.1 | async-start | bytes 1048576 | tf_op jit(solution)/shard_map/all_to_all | solution.py:25
  52.7 35.7 %copy-start = (f32[2048,128]{1,0:T(8,128)S(1)}, f32[2048,128]{1,0:T(8,128)}, u32[]{:S(2)}) copy-start(f32[2048,128]{1,0:T(8,128)} %param.12) | copy-start | bytes 3145732
  71.2 18.0 %copy-start.2 = (f32[2048]{0:T(1024)}, f32[2048]{0:T(1024)S(1)}, u32[]{:S(2)}) copy-start(f32[2048]{0:T(1024)S(1)} %add.50) | copy-start | bytes 24580
  75.4 26.7 %all-to-all-start.3 = ((f32[64,1,64]{2,1,0:T(1,128)}), f32[64,1,64]{2,1,0:T(1,128)S(1)}, u32[]{:S(2)}, u32[]{:S(2)}) async-start(f32[64,1,64]{2,1,0:T(1,128)} %all_to_all.18), calls=%async_computation.3 | async-start | bytes 65536 | tf_op jit(solution)/shard_map/all_to_all | solution.py:32
  89.2 12.9 %copy-start.1 = (f32[2048,128]{1,0:T(8,128)}, f32[2048,128]{1,0:T(8,128)S(1)}, u32[]{:S(2)}) copy-start(f32[2048,128]{1,0:T(8,128)S(1)} %divide_add_fusion) | copy-start | bytes 3145732
  102.1 10.5 %copy-start.8 = (f32[64]{0:T(128)S(1)}, f32[64]{0:T(128)}, u32[]{:S(2)}) copy-start(f32[64]{0:T(128)} %param.17) | copy-start | bytes 772
  102.1 60.1 %all-to-all-start.2 = ((f32[64,64,128]{2,1,0:T(8,128)}), f32[64,64,128]{2,1,0:T(8,128)S(1)}, u32[]{:S(2)}, u32[]{:S(2)}) async-start(f32[64,64,128]{2,1,0:T(8,128)} %bitcast.13), calls=%async_computation.2 | async-start | bytes 4194304 | tf_op jit(solution)/shard_map/all_to_all | solution.py:32
  112.6 49.8 %copy-start.3 = (f32[64,128]{1,0:T(8,128)S(1)}, f32[64,128]{1,0:T(8,128)}, u32[]{:S(2)}) copy-start(f32[64,128]{1,0:T(8,128)} %param.16) | copy-start | bytes 98308
  112.6 50.5 %copy-start.7 = (f32[64]{0:T(128)}, f32[64]{0:T(128)S(1)}, u32[]{:S(2)}) copy-start(f32[64]{0:T(128)S(1)} %add.54) | copy-start | bytes 772
where the time goes:
time: 164 us; the launch traced here: 163 us
  waiting for transfers between devices  68.4 us (42%)
  starting transfers between devices  47.3 us (29%)
  other arithmetic  40.3 us (25%)
  local copies, waits for them, and re-layouts  6.26 us (4%)
    all_to_all x2, waiting for transfers between devices, sum_at_owner(): parts = lax.all_to_all(in_blocks(x, dim, count), axis, 0, 0, tiled=True)  49.6 us
    all_to_all x2, starting transfers between devices, joined_exchange(): parts = lax.all_to_all(parts, axis, split_axis=0, concat_axis=0, tiled=True)  30.5 us
    scatter-add x2, other arithmetic, accumulate(): jnp.zeros((segments, values.shape[1]), jnp.float32).at[labels]  19.2 us
    all_to_all x2, waiting for transfers between devices, joined_exchange(): parts = lax.all_to_all(parts, axis, split_axis=0, concat_axis=0, tiled=True)  18.7 us
    scatter-add x2, other arithmetic, accumulate(): member_counts = jnp.zeros((segments,), jnp.float32).at[labels].add(jnp.on...  17.2 us
    all_to_all x2, starting transfers between devices, sum_at_owner(): parts = lax.all_to_all(in_blocks(x, dim, count), axis, 0, 0, tiled=True)  16.7 us
  transfers between devices with their start and end apart: 4, of which 3 were waited for; matrix products, arithmetic and copies ran while one was open for 25% of the time, Pallas kernels for 0%

commit v1 on v0

v1 whole, which is shorter than its diff:
```python
import functools

import jax
import jax.numpy as jnp
from jax import lax
from jax.experimental import pallas as pl
from jax.experimental.pallas import tpu as pltpu
from jax.sharding import Mesh, PartitionSpec as P

F32 = jnp.float32
BF16 = jnp.bfloat16
LANES = 128
BLOCK = 256


def iota(shape, dim):
    return lax.broadcasted_iota(jnp.int32, shape, dim)


def onehot(mask):
    return jnp.where(mask, 1.0, 0.0).astype(BF16)


def matmul(a, b):
    return lax.dot_general(a, b, (((1,), (0,)), ((), ())), preferred_element_type=F32)


def halves(x):
    high = x.astype(BF16)
    return high, (x - high.astype(F32)).astype(BF16)


def pack_kernel(empty, rows_ref, owner_ref, slot_ref, oc_ref, sc_ref, out_ref):
    batch, width = rows_ref.shape
    shards = batch
    groups = width // LANES
    lane = iota((shards, batch), 1)
    named = owner_ref[...] == iota((shards, batch), 0)
    first = jnp.min(jnp.where(named, lane.astype(F32), float(batch)), axis=1, keepdims=True)
    sel0 = lane.astype(F32) == first
    sel1 = jnp.logical_and(named, jnp.logical_not(sel0))
    slot = slot_ref[...].astype(F32)

    def label(sel):
        one = jnp.sum(jnp.where(sel, 1.0, 0.0), axis=1, keepdims=True)
        at = jnp.sum(jnp.where(sel, slot, 0.0), axis=1, keepdims=True)
        return at + (1.0 - one) * empty

    sel = jnp.concatenate([onehot(sel0), onehot(sel1)], axis=0)
    rows = rows_ref[...]
    high = rows.astype(BF16)
    rest = rows - high.astype(F32)
    mid, low = halves(rest)
    got = matmul(sel, high) + matmul(sel, mid) + matmul(sel, low)
    members = oc_ref.shape[1]
    a = onehot(oc_ref[...] == iota((shards, members), 0))
    b = onehot(sc_ref[...] + (LANES - shards) == iota((LANES, members), 0))
    hits = lax.dot_general(a, b, (((1,), (1,)), ((), ())), preferred_element_type=F32)
    where = iota((shards, LANES), 1)
    meta = jnp.where(where == 0, label(sel0), jnp.where(where == 1, label(sel1), hits))
    for z in range(groups):
        at = pl.ds(z * shards, shards)
        cols = slice(z * LANES, (z + 1) * LANES)
        out_ref[at, 0:LANES] = got[:shards, cols]
        out_ref[at, LANES : 2 * LANES] = got[shards:, cols]
        out_ref[at, 2 * LANES : 3 * LANES] = meta


def partial_sums(ids, parts_ref, out_ref):
    rows, members = out_ref.shape[0], parts_ref.shape[0]

    def step(i, carry):
        at = pl.multiple_of(i * BLOCK, BLOCK)
        hot = onehot(ids - at == iota((BLOCK, members), 0))
        both = matmul(hot, parts_ref[...])
        out_ref[pl.ds(at, BLOCK), :] = both[:, :LANES] + both[:, LANES:]
        return carry

    lax.fori_loop(0, rows // BLOCK, step, 0, unroll=2)


def ids_of(oc_ref, sc_ref, core, width):
    owner = oc_ref[...]
    ids = lax.shift_right_logical(owner, 1) * width + sc_ref[...]
    return jnp.where(jnp.bitwise_and(owner, 1) == core, ids, -1)


def move_kernel(
    width, core_ref, got_ref, cent_ref, counts_ref, oc_ref, sc_ref,
    moved_ref, new_counts_ref, send_ref, parts_ref, hits_ref,
):
    sources = got_ref.shape[0]
    lower = cent_ref.shape[0]
    meta = got_ref[:, 2 * LANES : 3 * LANES]
    hits_ref[...] = jnp.sum(meta[:width], axis=0, keepdims=True)
    across = meta.T
    labels = jnp.concatenate([across[0:1, :], across[1:2, :]], axis=1).astype(jnp.int32)
    rows = jnp.concatenate([got_ref[:, 0:LANES], got_ref[:, LANES : 2 * LANES]], axis=0)
    high, low = halves(rows)
    rhs = jnp.concatenate([high, low, jnp.ones((2 * sources, LANES), BF16)], axis=1)
    eye = iota((LANES, LANES), 0) == iota((LANES, LANES), 1)
    for i in range(lower // BLOCK):
        at = i * BLOCK
        hot = onehot(labels - at == iota((BLOCK, 2 * sources), 0))
        both = matmul(hot, rhs)
        summed = both[:, :LANES] + both[:, LANES : 2 * LANES]
        members = both[:, 2 * LANES :]
        old = cent_ref[at : at + BLOCK, :]
        total = counts_ref[at : at + BLOCK, :] + members
        moved = old + (summed - members * old) / total
        moved_ref[at : at + BLOCK, :] = moved
        high_m, low_m = halves(moved)
        parts_ref[at : at + BLOCK, :LANES] = high_m
        parts_ref[at : at + BLOCK, LANES:] = low_m
        for j in range(BLOCK // LANES):
            block = jnp.where(eye, total[j * LANES : (j + 1) * LANES], 0.0)
            row = i * (BLOCK // LANES) + j
            new_counts_ref[row : row + 1, :] = jnp.sum(block, axis=0, keepdims=True)
    partial_sums(ids_of(oc_ref, sc_ref, 1 - core_ref[0], width), parts_ref, send_ref)


def keep_kernel(width, core_ref, parts_ref, oc_ref, sc_ref, keep_ref):
    partial_sums(ids_of(oc_ref, sc_ref, core_ref[0], width), parts_ref, keep_ref)


VMEM = pl.BlockSpec(memory_space=pltpu.VMEM)
SMEM = pl.BlockSpec(memory_space=pltpu.SMEM)
PARAMS = pltpu.CompilerParams(vmem_limit_bytes=40 * 1024 * 1024)


def call(kernel, ins, outs, flops, nbytes, name):
    return pl.pallas_call(
        kernel,
        in_specs=ins,
        out_specs=[VMEM] * len(outs),
        out_shape=[jax.ShapeDtypeStruct(s, d) for s, d in outs],
        compiler_params=PARAMS,
        cost_estimate=pl.CostEstimate(flops=flops, bytes_accessed=nbytes, transcendentals=0),
        name=name,
    )


def body(rows_data, owner_rows, slot_rows, centroids, counts, owner_cent, slot_cent, upper, upper_counts):
    everyone = ("rows", "cx", "x", "core")
    groups = lax.axis_size("rows")
    shards = lax.axis_size(("cx", "x", "core"))
    batch = rows_data.shape[0]
    lower = centroids.shape[0]
    width = upper.shape[0]
    core = lax.axis_index("core").astype(jnp.int32).reshape(1)
    oc = owner_cent.reshape(1, lower)
    sc = slot_cent.reshape(1, lower)
    sent = 3 * LANES
    (packed,) = call(
        functools.partial(pack_kernel, lower),
        [VMEM] * 5,
        [((groups * shards, sent), F32)],
        10**8, 10**6, "pack",
    )(rows_data, owner_rows.reshape(1, batch), slot_rows.reshape(1, batch), oc, sc)
    got = lax.all_to_all(packed, everyone, 0, 0, tiled=True)
    wide_counts = jnp.broadcast_to(counts[:, None], (lower, LANES))
    half = width * shards // 2
    moved, new_counts, send, parts, hits = call(
        functools.partial(move_kernel, width),
        [SMEM] + [VMEM] * 5,
        [((lower, LANES), F32), ((lower // LANES, LANES), F32), ((half, LANES), F32), ((lower, 2 * LANES), BF16), ((1, LANES), F32)],
        4 * 10**9, 4 * 10**6, "move",
    )(core, got, centroids, wide_counts, oc, sc)
    arrived = lax.ppermute(send, "core", [(0, 1), (1, 0)])
    (keep,) = call(
        functools.partial(keep_kernel, width),
        [SMEM] + [VMEM] * 3,
        [((half, LANES), F32)],
        2 * 10**9, 2 * 10**6, "keep",
    )(core, parts, oc, sc)
    pair = (keep + arrived).reshape(shards // 2, width, LANES)
    pieces = lax.all_to_all(pair, ("cx", "x"), 0, 0, tiled=True)
    upper_summed = jnp.sum(pieces, axis=0)
    upper_members = hits[0, LANES - width :]
    new_upper_counts = upper_counts + upper_members
    new_upper = upper + (upper_summed - upper_members[:, None] * upper) / new_upper_counts[:, None]
    return moved, new_counts.reshape(lower), new_upper, new_upper_counts


def solution(mesh):
    groups, outer, inner = mesh.devices.shape
    fine = Mesh(mesh.devices.reshape(groups, outer, inner // 2, 2), ("rows", "cx", "x", "core"))
    everyone = ("rows", "cx", "x", "core")
    plane = ("cx", "x", "core")
    return jax.shard_map(
        body,
        mesh=fine,
        in_specs=(
            P(everyone, None), P(everyone, None), P(everyone),
            P(plane, "rows"), P(plane), P(plane, None), P(plane),
            P(plane, "rows"), P(plane),
        ),
        out_specs=(P(plane, "rows"), P(plane), P(plane, "rows"), P(plane)),
        check_vma=False,
    )
```

time: 164 us -> 103 us (0.63)
  other arithmetic: 40.3 us -> 1.93 us
  starting transfers between devices: 47.3 us -> 29.1 us
  waiting for transfers between devices: 68.4 us -> 54.7 us
  Pallas kernels: 0 us -> 9.12 us
    scatter-add x4 -> x0, other arithmetic: 36.3 us -> none  [the longest x2 19.2 us: accumulate(): jnp.zeros((segments, values.shape[1]), jnp.float32).at[labels]]
    all_to_all x4 -> x2, starting transfers between devices: 47.3 us -> 26.1 us  [the longest x1 22.2 us: body(): got = lax.all_to_all(packed, everyone, 0, 0, tiled=True)]
    all_to_all x4 -> x2, waiting for transfers between devices: 68.4 us -> 54.7 us  [the longest x1 27.4 us: body(): got = lax.all_to_all(packed, everyone, 0, 0, tiled=True)]
    pallas_call x0 -> x3, Pallas kernels: none -> 9.12 us  [the longest x1 5.69 us: body(): call(functools.partial(move_kernel, width), [SMEM] + [VMEM] * 5, [((lower...]
    unnamed x19 -> x25, local copies, waits for them, and re-layouts: 0.15 us -> 4.65 us
    ppermute x0 -> x1, starting transfers between devices: none -> 2.99 us  [body(): arrived = lax.ppermute(send, 'core', [(0, 1), (1, 0)])]
    scatter x2 -> x0, local copies, waits for them, and re-layouts: 2.26 us -> none  [the longest x1 1.36 us: bucket(): jnp.zeros((shards * capacity, values.shape[1]), values.dtype).at[target]]
  transfers between devices with their start and end apart: 4 -> 3, of which waited for: 3 -> 2; matrix products, arithmetic and copies ran while one was open for 25% -> 0% of each run, Pallas kernels for 0% -> 3%
where the time goes in v1:
time: 103 us; the launch traced here: 102 us
  waiting for transfers between devices  54.7 us (53%)
  starting transfers between devices  29.1 us (28%)
  Pallas kernels  9.12 us (9%)
  local copies, waits for them, and re-layouts  6.74 us (7%)
  other arithmetic  1.93 us (2%)
    all_to_all x1, waiting for transfers between devices, body(): got = lax.all_to_all(packed, everyone, 0, 0, tiled=True)  27.4 us
    all_to_all x1, waiting for transfers between devices, body(): pieces = lax.all_to_all(pair, ('cx', 'x'), 0, 0, tiled=True)  27.3 us
    all_to_all x1, starting transfers between devices, body(): got = lax.all_to_all(packed, everyone, 0, 0, tiled=True)  22.2 us
    pallas_call x1, Pallas kernels, body(): call(functools.partial(move_kernel, width), [SMEM] + [VMEM] * 5, [((lower...  5.69 us
    unnamed x25, local copies, waits for them, and re-layouts  4.65 us
    all_to_all x1, starting transfers between devices, body(): pieces = lax.all_to_all(pair, ('cx', 'x'), 0, 0, tiled=True)  3.93 us
    ppermute x1, starting transfers between devices, body(): arrived = lax.ppermute(send, 'core', [(0, 1), (1, 0)])  2.99 us
    pallas_call x1, Pallas kernels, body(): call(functools.partial(keep_kernel, width), [SMEM] + [VMEM] * 3, [((half,...  2.85 us
  transfers between devices with their start and end apart: 3, of which 2 were waited for; matrix products, arithmetic and copies ran while one was open for 0% of the time, Pallas kernels for 3%

profile of v1, /device:TPU:1, one launch (start us, length us, event | category | flops | bytes accessed | tf_op | source)
XLA Modules:
  0.0 102.3 jit_solution(9642013481390808529)
XLA Ops:
  0.6 0.0 copy-start.5
  0.6 0.0 copy-start.6
  0.7 0.6 copy-done.5
  1.3 0.0 copy-done.6
  1.3 0.0 copy-start
  1.3 0.9 copy-done
  2.3 0.0 copy-start.1
  2.3 0.7 copy-done.1
  3.0 0.0 copy-start.3
  3.0 0.7 copy-done.3
  3.6 0.6 pack.1
  4.2 1.7 %copy.13 = f32[512,1,384]{2,1,0:T(1,128)} copy(f32[512,1,384]{2,0,1:T(8,128)S(1)} %bitcast.15) | data formatting | bytes 1572864 | tf_op jit(solution)/shard_map/all_to_all | solution.py:160
  5.9 22.2 %all-to-all-start = ((f32[512,1,384]{2,1,0:T(1,128)}), f32[512,1,384]{2,1,0:T(1,128)S(1)}, u32[]{:S(2)}, u32[]{:S(2)}) async-start(f32[512,1,384]{2,1,0:T(1,128)} %copy.13), calls=%async_computation | async-start | bytes 1572864 | tf_op jit(solution)/shard_map/all_to_all | solution.py:160
  28.1 0.0 copy-start.7
  28.1 27.4 %all-to-all-done = f32[512,1,384]{2,1,0:T(1,128)S(1)} async-done(((f32[512,1,384]{2,1,0:T(1,128)}), f32[512,1,384]{2,1,0:T(1,128)S(1)}, u32[]{:S(2)}, u32[]{:S(2)}) %all-to-all-start) | async-done | bytes 786464 | tf_op jit(solution)/shard_map/all_to_all | solution.py:160
  55.5 0.0 copy-start.9
  55.5 0.1 copy.16
  55.6 0.6 copy-done.9
  56.2 0.0 copy-start.2
  56.2 0.0 copy-start.4
  56.2 0.3 broadcast_in_dim.2.counts_ref
  56.5 0.0 copy-done.7
  56.5 0.4 copy-done.2
  56.9 0.0 copy-done.4
  56.9 5.7 %move.1 = (f32[2048,128]{1,0:T(8,128)}, f32[16,128]{1,0:T(8,128)}, f32[2048,128]{1,0:T(8,128)S(1)}, bf16[2048,256]{1,0:T(8,128)(2,1)S(1)}, f32[1,128]{1,0:T(1,128)S(1)}) custom-call(s32[1]{0:T(128)} %bitcast.core_ref, f32[512,384]{1,0:T(8,128)S(1)} %bitcast.16, f32[2048,128]{1,0:T(8,128)S(1)} %copy-done.7, f32[2048,128]{1,0:T(8,128)S(1)} %broadcast_in_dim.2.counts_ref, ...), custom_call_target="tpu_custom_call" | custom-call | flops 4000000000 | bytes 4000000 | tf_op jit(solution)/shard_map/move/pallas_call | solution.py:163
  62.6 3.0 %collective-permute-start = (f32[2048,128]{1,0:T(8,128)S(1)}, f32[2048,128]{1,0:T(8,128)S(1)}, u32[]{:S(2)}, u32[]{:S(2)}) collective-permute-start(f32[2048,128]{1,0:T(8,128)S(1)} %get-tuple-element.12), channel_id=1, source_target_pairs={{0,1},{1,0},{2,3},{3,2},{4,5},{5,4},{6,7},{7,6},{8,9},{9,8},{10,11... | collective-permute-start | bytes 3145736 | tf_op jit(solution)/shard_map/ppermute | solution.py:169
  65.6 2.9 %keep.1 = f32[2048,128]{1,0:T(8,128)S(1)} custom-call(s32[1]{0:T(128)} %bitcast.core_ref, bf16[2048,256]{1,0:T(8,128)(2,1)S(1)} %get-tuple-element.11.parts_ref, s32[1,2048]{1,0:T(1,128)S(1)} %bitcast.19, s32[1,2048]{1,0:T(1,128)S(1)} %bitcast.22), custom_call_target="tpu_custom_call" | custom-call | flops 2000000000 | bytes 2000000 | tf_op jit(solution)/shard_map/keep/pallas_call | solution.py:170
  68.5 0.0 collective-permute-done
  68.5 1.1 %add.9 = f32[2048,128]{1,0:T(8,128)} add(f32[2048,128]{1,0:T(8,128)S(1)} %keep.1, f32[2048,128]{1,0:T(8,128)S(1)} %collective-permute-done) | non-fusion elementwise | flops 262144 | bytes 3145728 | tf_op jit(solution)/shard_map/add | solution.py:176
  69.6 3.9 %all-to-all-start.1 = ((f32[32,64,128]{2,1,0:T(8,128)}), f32[32,64,128]{2,1,0:T(8,128)S(1)}, u32[]{:S(2)}, u32[]{:S(2)}) async-start(f32[32,64,128]{2,1,0:T(8,128)} %bitcast.7), calls=%async_computation.1 | async-start | bytes 2097152 | tf_op jit(solution)/shard_map/all_to_all | solution.py:177
  73.5 0.0 copy-start.11
  73.5 0.1 slice_bitcast_fusion
  73.6 0.6 copy-done.11
  74.2 0.1 fusion
  74.2 0.0 copy-start.10
  74.2 0.0 copy-start.8
  74.2 27.3 %all-to-all-done.1 = f32[32,64,128]{2,1,0:T(8,128)S(1)} async-done(((f32[32,64,128]{2,1,0:T(8,128)}), f32[32,64,128]{2,1,0:T(8,128)S(1)}, u32[]{:S(2)}, u32[]{:S(2)}) %all-to-all-start.1) | async-done | bytes 1048608 | tf_op jit(solution)/shard_map/all_to_all | solution.py:177
  101.5 0.1 reduce_sum.9
  101.6 0.0 copy-done.10
  101.6 0.0 copy-done.8
  101.6 0.7 divide_add_fusion
Async XLA Ops:
  0.6 0.7 copy-start.5
  0.6 0.7 copy-start.6
  1.3 0.9 copy-start
  2.3 0.7 copy-start.1
  3.0 0.7 copy-start.3
  5.9 49.6 %all-to-all-start = ((f32[512,1,384]{2,1,0:T(1,128)}), f32[512,1,384]{2,1,0:T(1,128)S(1)}, u32[]{:S(2)}, u32[]{:S(2)}) async-start(f32[512,1,384]{2,1,0:T(1,128)} %copy.13), calls=%async_computation | async-start | bytes 1572864 | tf_op jit(solution)/shard_map/all_to_all | solution.py:160
  28.1 28.5 %copy-start.7 = (f32[2048,128]{1,0:T(8,128)S(1)}, f32[2048,128]{1,0:T(8,128)}, u32[]{:S(2)}) copy-start(f32[2048,128]{1,0:T(8,128)} %cent_ref.1) | copy-start | bytes 3145732
  55.5 0.7 copy-start.9
  56.2 0.7 copy-start.2
  56.2 0.7 copy-start.4
  62.6 5.9 %collective-permute-start = (f32[2048,128]{1,0:T(8,128)S(1)}, f32[2048,128]{1,0:T(8,128)S(1)}, u32[]{:S(2)}, u32[]{:S(2)}) collective-permute-start(f32[2048,128]{1,0:T(8,128)S(1)} %get-tuple-element.12), channel_id=1, source_target_pairs={{0,1},{1,0},{2,3},{3,2},{4,5},{5,4},{6,7},{7,6},{8,9},{9,8},{10,11... | collective-permute-start | bytes 3145736 | tf_op jit(solution)/shard_map/ppermute | solution.py:169
  69.6 32.0 %all-to-all-start.1 = ((f32[32,64,128]{2,1,0:T(8,128)}), f32[32,64,128]{2,1,0:T(8,128)S(1)}, u32[]{:S(2)}, u32[]{:S(2)}) async-start(f32[32,64,128]{2,1,0:T(8,128)} %bitcast.7), calls=%async_computation.1 | async-start | bytes 2097152 | tf_op jit(solution)/shard_map/all_to_all | solution.py:177
  73.5 0.7 copy-start.11
  74.2 27.4 %copy-start.10 = (f32[64]{0:T(128)}, f32[64]{0:T(128)S(1)}, u32[]{:S(2)}) copy-start(f32[64]{0:T(128)S(1)} %fusion) | copy-start | bytes 772
  74.2 27.4 %copy-start.8 = (f32[64,128]{1,0:T(8,128)S(1)}, f32[64,128]{1,0:T(8,128)}, u32[]{:S(2)}) copy-start(f32[64,128]{1,0:T(8,128)} %param.16) | copy-start | bytes 98308

commit v2 on v1

v2 whole, which is shorter than its diff:
```python
import functools

import jax
import jax.numpy as jnp
from jax import lax
from jax.experimental import pallas as pl
from jax.experimental.pallas import tpu as pltpu
from jax.sharding import Mesh, PartitionSpec as P

F32 = jnp.float32
BF16 = jnp.bfloat16
LANES = 128
BLOCK = 256
PARTS = 3


def iota(shape, dim):
    return lax.broadcasted_iota(jnp.int32, shape, dim)


def onehot(mask):
    return jnp.where(mask, 1.0, 0.0).astype(BF16)


def matmul(a, b):
    return lax.dot_general(a, b, (((1,), (0,)), ((), ())), preferred_element_type=F32)


def halves(x):
    high = x.astype(BF16)
    return high, (x - high.astype(F32)).astype(BF16)


def columns(row):
    return jnp.broadcast_to(row, (LANES, LANES)).T


def pack_kernel(
    empty, rows_hbm, owner_hbm, slot_hbm, oc_hbm, sc_hbm, out_ref,
    rows_ref, owner_ref, slot_ref, oc_ref, sc_ref, sems,
):
    pairs = [
        (owner_hbm, owner_ref), (slot_hbm, slot_ref), (oc_hbm, oc_ref), (sc_hbm, sc_ref), (rows_hbm, rows_ref),
    ]
    copies = [pltpu.make_async_copy(src, dst, sems.at[i]) for i, (src, dst) in enumerate(pairs)]
    for copy in copies:
        copy.start()
    for copy in copies[:4]:
        copy.wait()
    batch, width = rows_ref.shape
    shards = batch
    groups = width // LANES
    lane = iota((shards, batch), 1)
    named = owner_ref[...] == iota((shards, batch), 0)
    first = jnp.min(jnp.where(named, lane.astype(F32), float(batch)), axis=1, keepdims=True)
    sel0 = lane.astype(F32) == first
    sel1 = jnp.logical_and(named, jnp.logical_not(sel0))
    slot = slot_ref[...].astype(F32)

    def label(sel):
        return jnp.sum(jnp.where(sel, slot - empty, 0.0), axis=1, keepdims=True) + empty

    members = oc_ref.shape[1]
    a = onehot(oc_ref[...] == iota((shards, members), 0))
    b = onehot(sc_ref[...] + (LANES - shards) == iota((LANES, members), 0))
    hits = lax.dot_general(a, b, (((1,), (1,)), ((), ())), preferred_element_type=F32)
    where = iota((shards, LANES), 1)
    meta = jnp.where(where == 0, label(sel0), jnp.where(where == 1, label(sel1), hits))
    for z in range(groups):
        out_ref[pl.ds(z * shards * PARTS + 2, shards, stride=PARTS), :] = meta
    sel = jnp.concatenate([onehot(sel0), onehot(sel1)], axis=0)
    copies[4].wait()
    rows = rows_ref[...]
    high = rows.astype(BF16)
    mid, low = halves(rows - high.astype(F32))
    got = matmul(sel, high) + matmul(sel, mid) + matmul(sel, low)
    for z in range(groups):
        cols = slice(z * LANES, (z + 1) * LANES)
        for p in range(2):
            at = pl.ds(z * shards * PARTS + p, shards, stride=PARTS)
            out_ref[at, :] = got[p * shards : (p + 1) * shards, cols]


def side_kernel(counts_ref, upper_counts_ref, wide_ref, wide_upper_ref):
    for i in range(counts_ref.shape[0]):
        wide_ref[i * LANES : (i + 1) * LANES, :] = columns(counts_ref[i : i + 1, :])
    upper = upper_counts_ref[...]
    width = upper.shape[1]
    wide_upper_ref[...] = columns(jnp.concatenate([upper, jnp.zeros((1, LANES - width), F32)], axis=1))[:width]


def partial_sums(ids, parts_ref, out_ref):
    rows, members = out_ref.shape[0], parts_ref.shape[0]
    for at in range(0, rows, BLOCK):
        hot = onehot(ids - at == iota((BLOCK, members), 0))
        both = matmul(hot, parts_ref[...])
        out_ref[at : at + BLOCK, :] = both[:, :LANES] + both[:, LANES:]


def ids_of(oc_ref, sc_ref, core, width):
    owner = oc_ref[...]
    ids = lax.shift_right_logical(owner, 1) * width + sc_ref[...]
    return jnp.where(jnp.bitwise_and(owner, 1) == core, ids, -1)


def move_kernel(
    width, core_ref, got_ref, cent_ref, counts_ref, oc_ref, sc_ref,
    moved_hbm, new_counts_ref, send_ref, parts_ref, hits_ref, moved_ref, sem,
):
    sources = got_ref.shape[0] // PARTS
    lower = cent_ref.shape[0]
    part = [got_ref[pl.ds(i, sources, stride=PARTS), :] for i in range(PARTS)]
    meta = part[2]
    hits_ref[...] = jnp.sum(meta[:width], axis=0, keepdims=True)
    across = meta.T
    labels = jnp.concatenate([across[0:1, :], across[1:2, :]], axis=1).astype(jnp.int32)
    rows = jnp.concatenate(part[:2], axis=0)
    high, low = halves(rows)
    rhs = jnp.concatenate([high, low, jnp.ones((2 * sources, LANES), BF16)], axis=1)
    eye = iota((LANES, LANES), 0) == iota((LANES, LANES), 1)
    for i in range(lower // BLOCK):
        at = i * BLOCK
        hot = onehot(labels - at == iota((BLOCK, 2 * sources), 0))
        both = matmul(hot, rhs)
        summed = both[:, :LANES] + both[:, LANES : 2 * LANES]
        members = both[:, 2 * LANES :]
        old = cent_ref[at : at + BLOCK, :]
        total = counts_ref[at : at + BLOCK, :] + members
        moved = old + (summed - members * old) / total
        moved_ref[at : at + BLOCK, :] = moved
        high_m, low_m = halves(moved)
        parts_ref[at : at + BLOCK, :LANES] = high_m
        parts_ref[at : at + BLOCK, LANES:] = low_m
        for j in range(BLOCK // LANES):
            block = jnp.where(eye, total[j * LANES : (j + 1) * LANES], 0.0)
            row = i * (BLOCK // LANES) + j
            new_counts_ref[row : row + 1, :] = jnp.sum(block, axis=0, keepdims=True)
    copy = pltpu.make_async_copy(moved_ref, moved_hbm, sem)
    copy.start()
    partial_sums(ids_of(oc_ref, sc_ref, 1 - core_ref[0], width), parts_ref, send_ref)
    copy.wait()


def keep_kernel(
    width, core_ref, parts_ref, oc_ref, sc_ref, hits_ref, upper_counts_ref, keep_ref, members_ref, new_counts_ref,
):
    hits = hits_ref[...]
    members_ref[...] = columns(hits)[LANES - width :]
    new_counts_ref[...] = upper_counts_ref[...] + hits[:, LANES - width :]
    partial_sums(ids_of(oc_ref, sc_ref, core_ref[0], width), parts_ref, keep_ref)


def finish_kernel(pieces_ref, upper_ref, members_ref, counts_ref, out_ref):
    summed = jnp.sum(pieces_ref[...], axis=0)
    old, members = upper_ref[...], members_ref[...]
    out_ref[...] = old + (summed - members * old) / (counts_ref[...] + members)


VMEM = pl.BlockSpec(memory_space=pltpu.VMEM)
ANY = pl.BlockSpec(memory_space=pl.ANY)
SMEM = pl.BlockSpec(memory_space=pltpu.SMEM)


def call(kernel, ins, outs, flops, nbytes, name, out_specs=None, scratch=(), vmem=40):
    return pl.pallas_call(
        kernel,
        in_specs=ins,
        out_specs=out_specs or [VMEM] * len(outs),
        out_shape=[jax.ShapeDtypeStruct(s, d) for s, d in outs],
        scratch_shapes=list(scratch),
        compiler_params=pltpu.CompilerParams(vmem_limit_bytes=vmem * 1024 * 1024),
        cost_estimate=pl.CostEstimate(flops=flops, bytes_accessed=nbytes, transcendentals=0),
        name=name,
    )


def body(rows_data, owner_rows, slot_rows, centroids, counts, owner_cent, slot_cent, upper, upper_counts):
    everyone = ("rows", "cx", "x", "core")
    groups = lax.axis_size("rows")
    shards = lax.axis_size(("cx", "x", "core"))
    pairs = shards // 2
    devices = groups * shards
    batch, features = rows_data.shape
    lower = centroids.shape[0]
    width = upper.shape[0]
    core = lax.axis_index("core").astype(jnp.int32).reshape(1)
    oc = owner_cent.reshape(1, lower)
    sc = slot_cent.reshape(1, lower)
    half = width * pairs
    ints = lambda n: pltpu.VMEM((1, n), jnp.int32)
    (packed,) = call(
        functools.partial(pack_kernel, float(lower)),
        [ANY] * 5,
        [((devices * PARTS, LANES), F32)],
        10**8, 10**6, "pack", None,
        [pltpu.VMEM((batch, features), F32), ints(batch), ints(batch), ints(lower), ints(lower), pltpu.SemaphoreType.DMA((5,))],
        63,
    )(rows_data, owner_rows.reshape(1, batch), slot_rows.reshape(1, batch), oc, sc)
    got = lax.all_to_all(packed.reshape(devices, 1, PARTS * LANES), everyone, 0, 0, tiled=True)
    got = got.reshape(devices * PARTS, LANES)
    wide_counts, wide_upper = call(
        side_kernel,
        [VMEM] * 2,
        [((lower, LANES), F32), ((width, LANES), F32)],
        10**7, 10**6, "side",
    )(counts.reshape(lower // LANES, LANES), upper_counts.reshape(1, width))
    moved, new_counts, send, parts, hits = call(
        functools.partial(move_kernel, width),
        [SMEM] + [VMEM] * 5,
        [((lower, LANES), F32), ((lower // LANES, LANES), F32), ((half, LANES), F32), ((lower, 2 * LANES), BF16), ((1, LANES), F32)],
        4 * 10**9, 4 * 10**6, "move", [ANY] + [VMEM] * 4,
        [pltpu.VMEM((lower, LANES), F32), pltpu.SemaphoreType.DMA],
    )(core, got, centroids, wide_counts, oc, sc)
    arrived = lax.ppermute(send, "core", [(0, 1), (1, 0)])
    keep, members, new_upper_counts = call(
        functools.partial(keep_kernel, width),
        [SMEM] + [VMEM] * 5,
        [((half, LANES), F32), ((width, LANES), F32), ((1, width), F32)],
        2 * 10**9, 2 * 10**6, "keep",
    )(core, parts, oc, sc, hits, upper_counts.reshape(1, width))
    pair = (keep + arrived).reshape(pairs, width, LANES)
    pieces = lax.all_to_all(pair, ("cx", "x"), 0, 0, tiled=True)
    (new_upper,) = call(
        finish_kernel,
        [VMEM] * 4,
        [((width, LANES), F32)],
        10**6, 10**6, "finish",
    )(pieces, upper, members, wide_upper)
    return moved, new_counts.reshape(lower), new_upper, new_upper_counts.reshape(width)


def solution(mesh):
    groups, outer, inner = mesh.devices.shape
    fine = Mesh(mesh.devices.reshape(groups, outer, inner // 2, 2), ("rows", "cx", "x", "core"))
    everyone = ("rows", "cx", "x", "core")
    plane = ("cx", "x", "core")
    return jax.shard_map(
        body,
        mesh=fine,
        in_specs=(
            P(everyone, None), P(everyone, None), P(everyone),
            P(plane, "rows"), P(plane), P(plane, None), P(plane),
            P(plane, "rows"), P(plane),
        ),
        out_specs=(P(plane, "rows"), P(plane), P(plane, "rows"), P(plane)),
        check_vma=False,
    )
```

time: 103 us -> 96 us (0.932)
  blocking collectives: 0 us -> 30.4 us
  waiting for transfers between devices: 54.7 us -> 26.4 us
  local copies, waits for them, and re-layouts: 6.74 us -> 0.7 us
  starting transfers between devices: 29.1 us -> 25.2 us
  Pallas kernels: 9.12 us -> 11.6 us
  other arithmetic: 1.93 us -> 0.11 us
    all_to_all x0 -> x1, blocking collectives: none -> 30.4 us  [body(): pieces = lax.all_to_all(pair, ('cx', 'x'), 0, 0, tiled=True)]
    all_to_all x2 -> x1, waiting for transfers between devices: 54.7 us -> 26.4 us  [body(): lax.all_to_all(packed.reshape(devices, 1, PARTS * LANES), everyone, 0, 0,...]
    unnamed x25 -> x12, local copies, waits for them, and re-layouts: 4.65 us -> 0.7 us
    all_to_all x2 -> x1, starting transfers between devices: 26.1 us -> 22.2 us  [body(): lax.all_to_all(packed.reshape(devices, 1, PARTS * LANES), everyone, 0, 0,...]
    pallas_call x2 -> x4, Pallas kernels: 3.42 us -> 6.31 us  [the longest x1 2.72 us: body(): call(functools.partial(keep_kernel, width), [SMEM] + [VMEM] * 5, [((half,...]
    add x3 -> x1, other arithmetic: 1.86 us -> 0.11 us  [body(): pair = (keep + arrived).reshape(pairs, width, LANES)]
    all_to_all x1 -> x0, local copies, waits for them, and re-layouts: 1.69 us -> none  [body(): got = lax.all_to_all(packed, everyone, 0, 0, tiled=True)]
  transfers between devices with their start and end apart: 3 -> 2, of which waited for: 2 -> 1; matrix products, arithmetic and copies ran while one was open for 0% -> 0% of each run, Pallas kernels for 3% -> 3%
where the time goes in v2:
time: 96 us; the launch traced here: 95.1 us
  blocking collectives  30.4 us (32%)
  waiting for transfers between devices  26.4 us (28%)
  starting transfers between devices  25.2 us (26%)
  Pallas kernels  11.6 us (12%)
    all_to_all x1, blocking collectives, body(): pieces = lax.all_to_all(pair, ('cx', 'x'), 0, 0, tiled=True)  30.4 us
    all_to_all x1, waiting for transfers between devices, body(): lax.all_to_all(packed.reshape(devices, 1, PARTS * LANES), everyone, 0, 0,...  26.4 us
    all_to_all x1, starting transfers between devices, body(): lax.all_to_all(packed.reshape(devices, 1, PARTS * LANES), everyone, 0, 0,...  22.2 us
    pallas_call x1, Pallas kernels, body(): call(functools.partial(move_kernel, width), [SMEM] + [VMEM] * 5, [((lower...  5.31 us
    ppermute x1, starting transfers between devices, body(): arrived = lax.ppermute(send, 'core', [(0, 1), (1, 0)])  3.02 us
    pallas_call x1, Pallas kernels, body(): call(functools.partial(keep_kernel, width), [SMEM] + [VMEM] * 5, [((half,...  2.72 us
    pallas_call x1, Pallas kernels, body(): call(functools.partial(pack_kernel, float(lower)), [ANY] * 5, [((devices...  2.56 us
  transfers between devices with their start and end apart: 2, of which 1 were waited for; matrix products, arithmetic and copies ran while one was open for 0% of the time, Pallas kernels for 3%

profile of v2, /device:TPU:1, one launch (start us, length us, event | category | flops | bytes accessed | tf_op | source)
XLA Modules:
  0.0 95.1 jit_solution(17846644628602762877)
XLA Ops:
  0.6 2.6 %pack.1 = f32[1536,128]{1,0:T(8,128)} custom-call(f32[64,1024]{1,0:T(8,128)} %rows_hbm.1, s32[1,64]{1,0:T(1,128)} %bitcast.24, s32[1,64]{1,0:T(1,128)} %bitcast.25, s32[1,2048]{1,0:T(1,128)} %bitcast.13, s32[1,2048]{1,0:T(1,128)} %bitcast.16), custom_call_target="tpu_custom_call" | custom-call | flops 100000000 | bytes 1000000 | tf_op jit(solution)/shard_map/pack/pallas_call | solution.py:191
  3.2 0.0 copy-start.3
  3.2 22.2 %all-to-all-start = ((f32[512,1,384]{2,1,0:T(1,128)}), f32[512,1,384]{2,1,0:T(1,128)S(1)}, u32[]{:S(2)}, u32[]{:S(2)}) async-start(f32[512,1,384]{2,1,0:T(1,128)} %bitcast.23), calls=%async_computation | async-start | bytes 1572864 | tf_op jit(solution)/shard_map/all_to_all | solution.py:199
  25.4 0.0 copy-start.4
  25.4 0.0 copy-start.5
  25.4 0.7 copy-done.4
  26.1 0.0 copy-done.5
  26.1 0.0 copy-start.1
  26.1 0.0 copy-start.2
  26.1 0.3 side.1
  26.4 26.4 %all-to-all-done = f32[512,1,384]{2,1,0:T(1,128)S(1)} async-done(((f32[512,1,384]{2,1,0:T(1,128)}), f32[512,1,384]{2,1,0:T(1,128)S(1)}, u32[]{:S(2)}, u32[]{:S(2)}) %all-to-all-start) | async-done | bytes 786464 | tf_op jit(solution)/shard_map/all_to_all | solution.py:199
  52.8 0.0 copy-done.3
  52.8 0.0 copy-done.1
  52.8 0.0 copy-done.2
  52.8 5.3 %move.1 = (f32[2048,128]{1,0:T(8,128)}, f32[16,128]{1,0:T(8,128)}, f32[2048,128]{1,0:T(8,128)S(1)}, bf16[2048,256]{1,0:T(8,128)(2,1)S(1)}, f32[1,128]{1,0:T(1,128)S(1)}) custom-call(s32[1]{0:T(128)} %bitcast.core_ref, f32[1536,128]{1,0:T(8,128)S(1)} %bitcast.12, f32[2048,128]{1,0:T(8,128)S(1)} %copy-done.3, f32[2048,128]{1,0:T(8,128)S(1)} %get-tuple-element.14.counts_ref, ...), custom_call_target="tpu_custom_call" | custom-call | flops 4000000000 | bytes 4000000 | tf_op jit(solution)/shard_map/move/pallas_call | solution.py:207
  58.1 3.0 %collective-permute-start = (f32[2048,128]{1,0:T(8,128)S(1)}, f32[2048,128]{1,0:T(8,128)S(1)}, u32[]{:S(2)}, u32[]{:S(2)}) collective-permute-start(f32[2048,128]{1,0:T(8,128)S(1)} %get-tuple-element.20), channel_id=1, source_target_pairs={{0,1},{1,0},{2,3},{3,2},{4,5},{5,4},{6,7},{7,6},{8,9},{9,8},{10,11... | collective-permute-start | bytes 3145736 | tf_op jit(solution)/shard_map/ppermute | solution.py:214
  61.2 2.7 %keep.1 = (f32[2048,128]{1,0:T(8,128)S(1)}, f32[64,128]{1,0:T(8,128)S(1)}, f32[1,64]{1,0:T(1,128)}) custom-call(s32[1]{0:T(128)} %bitcast.core_ref, bf16[2048,256]{1,0:T(8,128)(2,1)S(1)} %get-tuple-element.17.parts_ref, s32[1,2048]{1,0:T(1,128)S(1)} %bitcast.15, s32[1,2048]{1,0:T(1,128)S(1)} %bitcast.18, f32[1,128]{1,0:T(1,128)S(1)} %get-tuple-element.18.hits_ref, ...), custom_call_target="tpu_custom_call" | custom-call | flops 2000000000 | bytes 2000000 | tf_op jit(solution)/shard_map/keep/pallas_call | solution.py:215
  63.9 0.0 collective-permute-done
  63.9 0.1 add.3
  64.0 0.0 copy-start
  64.0 30.4 %all_to_all.10.pieces_ref = f32[32,64,128]{2,1,0:T(8,128)S(1)} all-to-all(f32[32,64,128]{2,1,0:T(8,128)S(1)} %bitcast.22), channel_id=1, replica_groups=mesh['rows'=8,'cx'=8,'x'=4,'core'=2] {'cx','x'}, dimensions={0} | all-to-all | bytes 2097152 | tf_op jit(solution)/shard_map/all_to_all | solution.py:222
  94.4 0.0 copy-done
  94.4 0.7 finish.1
Async XLA Ops:
  3.2 49.6 %copy-start.3 = (f32[2048,128]{1,0:T(8,128)S(1)}, f32[2048,128]{1,0:T(8,128)}, u32[]{:S(2)}) copy-start(f32[2048,128]{1,0:T(8,128)} %cent_ref.1) | copy-start | bytes 3145732
  3.2 49.6 %all-to-all-start = ((f32[512,1,384]{2,1,0:T(1,128)}), f32[512,1,384]{2,1,0:T(1,128)S(1)}, u32[]{:S(2)}, u32[]{:S(2)}) async-start(f32[512,1,384]{2,1,0:T(1,128)} %bitcast.23), calls=%async_computation | async-start | bytes 1572864 | tf_op jit(solution)/shard_map/all_to_all | solution.py:199
  25.4 0.7 copy-start.4
  25.4 0.7 copy-start.5
  26.1 26.7 %copy-start.1 = (s32[2048,1]{0,1:T(1,128)S(1)}, s32[2048,1]{0,1:T(1,128)}, u32[]{:S(2)}) copy-start(s32[2048,1]{0,1:T(1,128)} %param.14) | copy-start | bytes 24580
  26.1 26.7 %copy-start.2 = (s32[2048]{0:T(1024)S(1)}, s32[2048]{0:T(1024)}, u32[]{:S(2)}) copy-start(s32[2048]{0:T(1024)} %param.15) | copy-start | bytes 24580
  58.1 5.7 %collective-permute-start = (f32[2048,128]{1,0:T(8,128)S(1)}, f32[2048,128]{1,0:T(8,128)S(1)}, u32[]{:S(2)}, u32[]{:S(2)}) collective-permute-start(f32[2048,128]{1,0:T(8,128)S(1)} %get-tuple-element.20), channel_id=1, source_target_pairs={{0,1},{1,0},{2,3},{3,2},{4,5},{5,4},{6,7},{7,6},{8,9},{9,8},{10,11... | collective-permute-start | bytes 3145736 | tf_op jit(solution)/shard_map/ppermute | solution.py:214
  64.0 30.4 %copy-start = (f32[64,128]{1,0:T(8,128)S(1)}, f32[64,128]{1,0:T(8,128)}, u32[]{:S(2)}) copy-start(f32[64,128]{1,0:T(8,128)} %upper_ref.1) | copy-start | bytes 98308

commit v3 on v2

--- a/solution.py
+++ b/solution.py
@@ -39,10 +39,10 @@
     empty, rows_hbm, owner_hbm, slot_hbm, oc_hbm, sc_hbm, out_ref,
     rows_ref, owner_ref, slot_ref, oc_ref, sc_ref, sems,
 ):
-    pairs = [
+    moves = [
         (owner_hbm, owner_ref), (slot_hbm, slot_ref), (oc_hbm, oc_ref), (sc_hbm, sc_ref), (rows_hbm, rows_ref),
     ]
-    copies = [pltpu.make_async_copy(src, dst, sems.at[i]) for i, (src, dst) in enumerate(pairs)]
+    copies = [pltpu.make_async_copy(src, dst, sems.at[i]) for i, (src, dst) in enumerate(moves)]
     for copy in copies:
         copy.start()
     for copy in copies[:4]:
@@ -50,8 +50,14 @@
     batch, width = rows_ref.shape
     shards = batch
     groups = width // LANES
+    pairs = shards // 2
+
+    def shard_at(shape):
+        at = iota(shape, 0)
+        return jnp.where(at < pairs, 2 * at, 2 * at - (shards - 1))
+
     lane = iota((shards, batch), 1)
-    named = owner_ref[...] == iota((shards, batch), 0)
+    named = owner_ref[...] == shard_at((shards, batch))
     first = jnp.min(jnp.where(named, lane.astype(F32), float(batch)), axis=1, keepdims=True)
     sel0 = lane.astype(F32) == first
     sel1 = jnp.logical_and(named, jnp.logical_not(sel0))
@@ -61,13 +67,18 @@
         return jnp.sum(jnp.where(sel, slot - empty, 0.0), axis=1, keepdims=True) + empty
 
     members = oc_ref.shape[1]
-    a = onehot(oc_ref[...] == iota((shards, members), 0))
+    a = onehot(oc_ref[...] == shard_at((shards, members)))
     b = onehot(sc_ref[...] + (LANES - shards) == iota((LANES, members), 0))
     hits = lax.dot_general(a, b, (((1,), (1,)), ((), ())), preferred_element_type=F32)
     where = iota((shards, LANES), 1)
     meta = jnp.where(where == 0, label(sel0), jnp.where(where == 1, label(sel1), hits))
+
+    def spots(core, z, part):
+        return pl.ds((core * groups + z) * pairs * PARTS + part, pairs, stride=PARTS)
+
     for z in range(groups):
-        out_ref[pl.ds(z * shards * PARTS + 2, shards, stride=PARTS), :] = meta
+        for core in range(2):
+            out_ref[spots(core, z, 2), :] = meta[core * pairs : (core + 1) * pairs]
     sel = jnp.concatenate([onehot(sel0), onehot(sel1)], axis=0)
     copies[4].wait()
     rows = rows_ref[...]
@@ -77,8 +88,9 @@
     for z in range(groups):
         cols = slice(z * LANES, (z + 1) * LANES)
         for p in range(2):
-            at = pl.ds(z * shards * PARTS + p, shards, stride=PARTS)
-            out_ref[at, :] = got[p * shards : (p + 1) * shards, cols]
+            for core in range(2):
+                at = p * shards + core * pairs
+                out_ref[spots(core, z, p), :] = got[at : at + pairs, cols]
 
 
 def side_kernel(counts_ref, upper_counts_ref, wide_ref, wide_upper_ref):
@@ -104,14 +116,16 @@
 
 
 def move_kernel(
-    width, core_ref, got_ref, cent_ref, counts_ref, oc_ref, sc_ref,
+    width, pairs, core_ref, got_ref, cent_ref, counts_ref, oc_ref, sc_ref,
     moved_hbm, new_counts_ref, send_ref, parts_ref, hits_ref, moved_ref, sem,
 ):
     sources = got_ref.shape[0] // PARTS
     lower = cent_ref.shape[0]
     part = [got_ref[pl.ds(i, sources, stride=PARTS), :] for i in range(PARTS)]
     meta = part[2]
-    hits_ref[...] = jnp.sum(meta[:width], axis=0, keepdims=True)
+    half = sources // 2
+    counted = meta[:pairs] + meta[half : half + pairs]
+    hits_ref[...] = jnp.sum(counted, axis=0, keepdims=True)
     across = meta.T
     labels = jnp.concatenate([across[0:1, :], across[1:2, :]], axis=1).astype(jnp.int32)
     rows = jnp.concatenate(part[:2], axis=0)
@@ -175,7 +189,7 @@
 
 
 def body(rows_data, owner_rows, slot_rows, centroids, counts, owner_cent, slot_cent, upper, upper_counts):
-    everyone = ("rows", "cx", "x", "core")
+    exchange = ("core", "rows", "cx", "x")
     groups = lax.axis_size("rows")
     shards = lax.axis_size(("cx", "x", "core"))
     pairs = shards // 2
@@ -196,7 +210,7 @@
         [pltpu.VMEM((batch, features), F32), ints(batch), ints(batch), ints(lower), ints(lower), pltpu.SemaphoreType.DMA((5,))],
         63,
     )(rows_data, owner_rows.reshape(1, batch), slot_rows.reshape(1, batch), oc, sc)
-    got = lax.all_to_all(packed.reshape(devices, 1, PARTS * LANES), everyone, 0, 0, tiled=True)
+    got = lax.all_to_all(packed.reshape(devices, 1, PARTS * LANES), exchange, 0, 0, tiled=True)
     got = got.reshape(devices * PARTS, LANES)
     wide_counts, wide_upper = call(
         side_kernel,
@@ -205,7 +219,7 @@
         10**7, 10**6, "side",
     )(counts.reshape(lower // LANES, LANES), upper_counts.reshape(1, width))
     moved, new_counts, send, parts, hits = call(
-        functools.partial(move_kernel, width),
+        functools.partial(move_kernel, width, pairs),
         [SMEM] + [VMEM] * 5,
         [((lower, LANES), F32), ((lower // LANES, LANES), F32), ((half, LANES), F32), ((lower, 2 * LANES), BF16), ((1, LANES), F32)],
         4 * 10**9, 4 * 10**6, "move", [ANY] + [VMEM] * 4,

time: 96 us -> 96 us (level)
  no operation moved by 1% of the time
where the time goes in v3:
time: 96 us; the launch traced here: 95.1 us
  blocking collectives  31.3 us (33%)
  waiting for transfers between devices  26.2 us (27%)
  starting transfers between devices  24.4 us (25%)
  Pallas kernels  11.6 us (12%)
    all_to_all x1, blocking collectives, body(): pieces = lax.all_to_all(pair, ('cx', 'x'), 0, 0, tiled=True)  31.3 us
    all_to_all x1, waiting for transfers between devices, body(): lax.all_to_all(packed.reshape(devices, 1, PARTS * LANES), exchange, 0, 0,...  26.2 us
    all_to_all x1, starting transfers between devices, body(): lax.all_to_all(packed.reshape(devices, 1, PARTS * LANES), exchange, 0, 0,...  22.2 us
    pallas_call x1, Pallas kernels, body(): call(functools.partial(move_kernel, width, pairs), [SMEM] + [VMEM] * 5, [...  5.32 us
    pallas_call x1, Pallas kernels, body(): call(functools.partial(keep_kernel, width), [SMEM] + [VMEM] * 5, [((half,...  2.72 us
    pallas_call x1, Pallas kernels, body(): call(functools.partial(pack_kernel, float(lower)), [ANY] * 5, [((devices...  2.56 us
    ppermute x1, starting transfers between devices, body(): arrived = lax.ppermute(send, 'core', [(0, 1), (1, 0)])  2.28 us
  transfers between devices with their start and end apart: 2, of which 1 were waited for; matrix products, arithmetic and copies ran while one was open for 0% of the time, Pallas kernels for 3%

profile of v3, /device:TPU:1, one launch (start us, length us, event | category | flops | bytes accessed | tf_op | source)
XLA Modules:
  0.0 95.1 jit_solution(7544173787198713057)
XLA Ops:
  0.6 2.6 %pack.1 = f32[1536,128]{1,0:T(8,128)} custom-call(f32[64,1024]{1,0:T(8,128)} %rows_hbm.1, s32[1,64]{1,0:T(1,128)} %bitcast.24, s32[1,64]{1,0:T(1,128)} %bitcast.25, s32[1,2048]{1,0:T(1,128)} %bitcast.13, s32[1,2048]{1,0:T(1,128)} %bitcast.16), custom_call_target="tpu_custom_call" | custom-call | flops 100000000 | bytes 1000000 | tf_op jit(solution)/shard_map/pack/pallas_call | solution.py:205
  3.2 0.0 copy-start.3
  3.2 22.2 %all-to-all-start = ((f32[512,1,384]{2,1,0:T(1,128)}), f32[512,1,384]{2,1,0:T(1,128)S(1)}, u32[]{:S(2)}, u32[]{:S(2)}) async-start(f32[512,1,384]{2,1,0:T(1,128)} %bitcast.23), calls=%async_computation | async-start | bytes 1572864 | tf_op jit(solution)/shard_map/all_to_all | solution.py:213
  25.4 0.0 copy-start.4
  25.4 0.0 copy-start.5
  25.4 0.7 copy-done.4
  26.1 0.0 copy-done.5
  26.1 0.0 copy-start.1
  26.1 0.0 copy-start.2
  26.1 0.3 side.1
  26.4 26.2 %all-to-all-done = f32[512,1,384]{2,1,0:T(1,128)S(1)} async-done(((f32[512,1,384]{2,1,0:T(1,128)}), f32[512,1,384]{2,1,0:T(1,128)S(1)}, u32[]{:S(2)}, u32[]{:S(2)}) %all-to-all-start) | async-done | bytes 786464 | tf_op jit(solution)/shard_map/all_to_all | solution.py:213
  52.6 0.0 copy-done.3
  52.6 0.0 copy-done.1
  52.6 0.0 copy-done.2
  52.6 5.3 %move.1 = (f32[2048,128]{1,0:T(8,128)}, f32[16,128]{1,0:T(8,128)}, f32[2048,128]{1,0:T(8,128)S(1)}, bf16[2048,256]{1,0:T(8,128)(2,1)S(1)}, f32[1,128]{1,0:T(1,128)S(1)}) custom-call(s32[1]{0:T(128)} %bitcast.core_ref, f32[1536,128]{1,0:T(8,128)S(1)} %bitcast.12, f32[2048,128]{1,0:T(8,128)S(1)} %copy-done.3, f32[2048,128]{1,0:T(8,128)S(1)} %get-tuple-element.14.counts_ref, ...), custom_call_target="tpu_custom_call" | custom-call | flops 4000000000 | bytes 4000000 | tf_op jit(solution)/shard_map/move/pallas_call | solution.py:221
  58.0 2.3 %collective-permute-start = (f32[2048,128]{1,0:T(8,128)S(1)}, f32[2048,128]{1,0:T(8,128)S(1)}, u32[]{:S(2)}, u32[]{:S(2)}) collective-permute-start(f32[2048,128]{1,0:T(8,128)S(1)} %get-tuple-element.20), channel_id=1, source_target_pairs={{0,1},{1,0},{2,3},{3,2},{4,5},{5,4},{6,7},{7,6},{8,9},{9,8},{10,11... | collective-permute-start | bytes 3145736 | tf_op jit(solution)/shard_map/ppermute | solution.py:228
  60.3 2.7 %keep.1 = (f32[2048,128]{1,0:T(8,128)S(1)}, f32[64,128]{1,0:T(8,128)S(1)}, f32[1,64]{1,0:T(1,128)}) custom-call(s32[1]{0:T(128)} %bitcast.core_ref, bf16[2048,256]{1,0:T(8,128)(2,1)S(1)} %get-tuple-element.17.parts_ref, s32[1,2048]{1,0:T(1,128)S(1)} %bitcast.15, s32[1,2048]{1,0:T(1,128)S(1)} %bitcast.18, f32[1,128]{1,0:T(1,128)S(1)} %get-tuple-element.18.hits_ref, ...), custom_call_target="tpu_custom_call" | custom-call | flops 2000000000 | bytes 2000000 | tf_op jit(solution)/shard_map/keep/pallas_call | solution.py:229
  63.0 0.0 collective-permute-done
  63.0 0.1 add.3
  63.1 0.0 copy-start
  63.1 31.3 %all_to_all.10.pieces_ref = f32[32,64,128]{2,1,0:T(8,128)S(1)} all-to-all(f32[32,64,128]{2,1,0:T(8,128)S(1)} %bitcast.22), channel_id=1, replica_groups=mesh['rows'=8,'cx'=8,'x'=4,'core'=2] {'cx','x'}, dimensions={0} | all-to-all | bytes 2097152 | tf_op jit(solution)/shard_map/all_to_all | solution.py:236
  94.4 0.0 copy-done
  94.4 0.7 finish.1
Async XLA Ops:
  3.2 49.4 %copy-start.3 = (f32[2048,128]{1,0:T(8,128)S(1)}, f32[2048,128]{1,0:T(8,128)}, u32[]{:S(2)}) copy-start(f32[2048,128]{1,0:T(8,128)} %cent_ref.1) | copy-start | bytes 3145732
  3.2 49.4 %all-to-all-start = ((f32[512,1,384]{2,1,0:T(1,128)}), f32[512,1,384]{2,1,0:T(1,128)S(1)}, u32[]{:S(2)}, u32[]{:S(2)}) async-start(f32[512,1,384]{2,1,0:T(1,128)} %bitcast.23), calls=%async_computation | async-start | bytes 1572864 | tf_op jit(solution)/shard_map/all_to_all | solution.py:213
  25.4 0.7 copy-start.4
  25.4 0.7 copy-start.5
  26.1 26.5 %copy-start.1 = (s32[2048,1]{0,1:T(1,128)S(1)}, s32[2048,1]{0,1:T(1,128)}, u32[]{:S(2)}) copy-start(s32[2048,1]{0,1:T(1,128)} %param.14) | copy-start | bytes 24580
  26.1 26.5 %copy-start.2 = (s32[2048]{0:T(1024)S(1)}, s32[2048]{0:T(1024)}, u32[]{:S(2)}) copy-start(s32[2048]{0:T(1024)} %param.15) | copy-start | bytes 24580
  58.0 5.0 %collective-permute-start = (f32[2048,128]{1,0:T(8,128)S(1)}, f32[2048,128]{1,0:T(8,128)S(1)}, u32[]{:S(2)}, u32[]{:S(2)}) collective-permute-start(f32[2048,128]{1,0:T(8,128)S(1)} %get-tuple-element.20), channel_id=1, source_target_pairs={{0,1},{1,0},{2,3},{3,2},{4,5},{5,4},{6,7},{7,6},{8,9},{9,8},{10,11... | collective-permute-start | bytes 3145736 | tf_op jit(solution)/shard_map/ppermute | solution.py:228
  63.1 31.3 %copy-start = (f32[64,128]{1,0:T(8,128)S(1)}, f32[64,128]{1,0:T(8,128)}, u32[]{:S(2)}) copy-start(f32[64,128]{1,0:T(8,128)} %upper_ref.1) | copy-start | bytes 98308

commit v4 on v2

--- a/solution.py
+++ b/solution.py
@@ -97,14 +97,21 @@
         out_ref[at : at + BLOCK, :] = both[:, :LANES] + both[:, LANES:]
 
 
-def ids_of(oc_ref, sc_ref, core, width):
+def ids_of(oc_ref, sc_ref, core, width, places):
     owner = oc_ref[...]
-    ids = lax.shift_right_logical(owner, 1) * width + sc_ref[...]
-    return jnp.where(jnp.bitwise_and(owner, 1) == core, ids, -1)
+    outer, inner, fold = places
+    x = jnp.bitwise_and(lax.shift_right_logical(owner, 1), inner - 1)
+    y = owner // (2 * inner)
+    low, high = jnp.bitwise_and(y, fold - 1), y // fold
+    first = x * outer + y
+    other = low * (inner * outer // fold) + high * inner + x
+    mine = jnp.bitwise_and(owner, 1)
+    ids = jnp.where(mine == 0, first, other) * width + sc_ref[...]
+    return jnp.where(mine == core, ids, -1)
 
 
 def move_kernel(
-    width, core_ref, got_ref, cent_ref, counts_ref, oc_ref, sc_ref,
+    width, places, core_ref, got_ref, cent_ref, counts_ref, oc_ref, sc_ref,
     moved_hbm, new_counts_ref, send_ref, parts_ref, hits_ref, moved_ref, sem,
 ):
     sources = got_ref.shape[0] // PARTS
@@ -137,17 +144,17 @@
             new_counts_ref[row : row + 1, :] = jnp.sum(block, axis=0, keepdims=True)
     copy = pltpu.make_async_copy(moved_ref, moved_hbm, sem)
     copy.start()
-    partial_sums(ids_of(oc_ref, sc_ref, 1 - core_ref[0], width), parts_ref, send_ref)
+    partial_sums(ids_of(oc_ref, sc_ref, 1 - core_ref[0], width, places), parts_ref, send_ref)
     copy.wait()
 
 
 def keep_kernel(
-    width, core_ref, parts_ref, oc_ref, sc_ref, hits_ref, upper_counts_ref, keep_ref, members_ref, new_counts_ref,
+    width, places, core_ref, parts_ref, oc_ref, sc_ref, hits_ref, upper_counts_ref, keep_ref, members_ref, new_counts_ref,
 ):
     hits = hits_ref[...]
     members_ref[...] = columns(hits)[LANES - width :]
     new_counts_ref[...] = upper_counts_ref[...] + hits[:, LANES - width :]
-    partial_sums(ids_of(oc_ref, sc_ref, core_ref[0], width), parts_ref, keep_ref)
+    partial_sums(ids_of(oc_ref, sc_ref, core_ref[0], width, places), parts_ref, keep_ref)
 
 
 def finish_kernel(pieces_ref, upper_ref, members_ref, counts_ref, out_ref):
@@ -174,16 +181,14 @@
     )
 
 
-def body(rows_data, owner_rows, slot_rows, centroids, counts, owner_cent, slot_cent, upper, upper_counts):
-    everyone = ("rows", "cx", "x", "core")
-    groups = lax.axis_size("rows")
-    shards = lax.axis_size(("cx", "x", "core"))
+def body(places, rows_data, owner_rows, slot_rows, centroids, counts, owner_cent, slot_cent, upper, upper_counts):
+    groups, shards = lax.axis_size("rows"), lax.axis_size("plane")
     pairs = shards // 2
     devices = groups * shards
     batch, features = rows_data.shape
     lower = centroids.shape[0]
     width = upper.shape[0]
-    core = lax.axis_index("core").astype(jnp.int32).reshape(1)
+    core = jnp.bitwise_and(lax.axis_index("plane"), 1).astype(jnp.int32).reshape(1)
     oc = owner_cent.reshape(1, lower)
     sc = slot_cent.reshape(1, lower)
     half = width * pairs
@@ -196,7 +201,7 @@
         [pltpu.VMEM((batch, features), F32), ints(batch), ints(batch), ints(lower), ints(lower), pltpu.SemaphoreType.DMA((5,))],
         63,
     )(rows_data, owner_rows.reshape(1, batch), slot_rows.reshape(1, batch), oc, sc)
-    got = lax.all_to_all(packed.reshape(devices, 1, PARTS * LANES), everyone, 0, 0, tiled=True)
+    got = lax.all_to_all(packed.reshape(devices, 1, PARTS * LANES), ("rows", "plane"), 0, 0, tiled=True)
     got = got.reshape(devices * PARTS, LANES)
     wide_counts, wide_upper = call(
         side_kernel,
@@ -205,21 +210,29 @@
         10**7, 10**6, "side",
     )(counts.reshape(lower // LANES, LANES), upper_counts.reshape(1, width))
     moved, new_counts, send, parts, hits = call(
-        functools.partial(move_kernel, width),
+        functools.partial(move_kernel, width, places),
         [SMEM] + [VMEM] * 5,
         [((lower, LANES), F32), ((lower // LANES, LANES), F32), ((half, LANES), F32), ((lower, 2 * LANES), BF16), ((1, LANES), F32)],
         4 * 10**9, 4 * 10**6, "move", [ANY] + [VMEM] * 4,
         [pltpu.VMEM((lower, LANES), F32), pltpu.SemaphoreType.DMA],
     )(core, got, centroids, wide_counts, oc, sc)
-    arrived = lax.ppermute(send, "core", [(0, 1), (1, 0)])
+    arrived = lax.ppermute(send, "plane", [(s, s ^ 1) for s in range(shards)])
     keep, members, new_upper_counts = call(
-        functools.partial(keep_kernel, width),
+        functools.partial(keep_kernel, width, places),
         [SMEM] + [VMEM] * 5,
         [((half, LANES), F32), ((width, LANES), F32), ((1, width), F32)],
         2 * 10**9, 2 * 10**6, "keep",
     )(core, parts, oc, sc, hits, upper_counts.reshape(1, width))
-    pair = (keep + arrived).reshape(pairs, width, LANES)
-    pieces = lax.all_to_all(pair, ("cx", "x"), 0, 0, tiled=True)
+    outer, inner, fold = places
+    at = lambda y, x, c: (y * inner + x) * 2 + c
+    near = [[at(y, x, 0) for x in range(inner)] for y in range(outer)]
+    near += [[at(h * fold + l, x, 1) for l in range(fold)] for h in range(outer // fold) for x in range(inner)]
+    far = [[at(y, x, 0) for y in range(outer)] for x in range(inner)]
+    far += [[at(h * fold + l, x, 1) for h in range(outer // fold) for x in range(inner)] for l in range(fold)]
+    pair = (keep + arrived).reshape(inner, outer * width, LANES)
+    merged = jnp.sum(lax.all_to_all(pair, "plane", 0, 0, axis_index_groups=near, tiled=True), axis=0)
+    merged = merged.reshape(outer, width, LANES)
+    pieces = lax.all_to_all(merged, "plane", 0, 0, axis_index_groups=far, tiled=True)
     (new_upper,) = call(
         finish_kernel,
         [VMEM] * 4,
@@ -231,17 +244,17 @@
 
 def solution(mesh):
     groups, outer, inner = mesh.devices.shape
-    fine = Mesh(mesh.devices.reshape(groups, outer, inner // 2, 2), ("rows", "cx", "x", "core"))
-    everyone = ("rows", "cx", "x", "core")
-    plane = ("cx", "x", "core")
+    fine = Mesh(mesh.devices.reshape(groups, outer * inner), ("rows", "plane"))
+    everyone = ("rows", "plane")
+    inner = inner // 2
     return jax.shard_map(
-        body,
+        functools.partial(body, (outer, inner, inner)),
         mesh=fine,
         in_specs=(
             P(everyone, None), P(everyone, None), P(everyone),
-            P(plane, "rows"), P(plane), P(plane, None), P(plane),
-            P(plane, "rows"), P(plane),
+            P("plane", "rows"), P("plane"), P("plane", None), P("plane"),
+            P("plane", "rows"), P("plane"),
         ),
-        out_specs=(P(plane, "rows"), P(plane), P(plane, "rows"), P(plane)),
+        out_specs=(P("plane", "rows"), P("plane"), P("plane", "rows"), P("plane")),
         check_vma=False,
     )

time: 96 us -> 96 us (level)
    all_to_all x1 -> x2, blocking collectives: 30.4 us -> 30.9 us  [the longest x1 17.2 us: body(): lax.all_to_all(pair, 'plane', 0, 0, axis_index_groups=near, tiled=True)]
where the time goes in v4:
time: 96 us; the launch traced here: 95.7 us
  blocking collectives  30.9 us (32%)
  waiting for transfers between devices  26.4 us (28%)
  starting transfers between devices  25.2 us (26%)
  Pallas kernels  11.6 us (12%)
    all_to_all x1, waiting for transfers between devices, body(): lax.all_to_all(packed.reshape(devices, 1, PARTS * LANES), ('rows', 'plane...  26.4 us
    all_to_all x1, starting transfers between devices, body(): lax.all_to_all(packed.reshape(devices, 1, PARTS * LANES), ('rows', 'plane...  22.2 us
    all_to_all x1, blocking collectives, body(): lax.all_to_all(pair, 'plane', 0, 0, axis_index_groups=near, tiled=True)  17.2 us
    all_to_all x1, blocking collectives, body(): lax.all_to_all(merged, 'plane', 0, 0, axis_index_groups=far, tiled=True)  13.8 us
    pallas_call x1, Pallas kernels, body(): call(functools.partial(move_kernel, width, places), [SMEM] + [VMEM] * 5,...  5.32 us
    ppermute x1, starting transfers between devices, body(): arrived = lax.ppermute(send, 'plane', [(s, s ^ 1) for s in range(shards)])  3.02 us
    pallas_call x1, Pallas kernels, body(): call(functools.partial(keep_kernel, width, places), [SMEM] + [VMEM] * 5,...  2.72 us
    pallas_call x1, Pallas kernels, body(): call(functools.partial(pack_kernel, float(lower)), [ANY] * 5, [((devices...  2.56 us
  transfers between devices with their start and end apart: 2, of which 1 were waited for; matrix products, arithmetic and copies ran while one was open for 0% of the time, Pallas kernels for 3%

profile of v4, /device:TPU:1, one launch (start us, length us, event | category | flops | bytes accessed | tf_op | source)
XLA Modules:
  0.0 95.7 jit_solution(7978957416846030094)
XLA Ops:
  0.6 2.6 %pack.1 = f32[1536,128]{1,0:T(8,128)} custom-call(f32[64,1024]{1,0:T(8,128)} %rows_hbm.1, s32[1,64]{1,0:T(1,128)} %bitcast.26, s32[1,64]{1,0:T(1,128)} %bitcast.27, s32[1,2048]{1,0:T(1,128)} %bitcast.14, s32[1,2048]{1,0:T(1,128)} %bitcast.17), custom_call_target="tpu_custom_call" | custom-call | flops 100000000 | bytes 1000000 | tf_op jit(solution)/shard_map/pack/pallas_call | solution.py:196
  3.2 0.0 copy-start.3
  3.2 22.2 %all-to-all-start = ((f32[512,1,384]{2,1,0:T(1,128)}), f32[512,1,384]{2,1,0:T(1,128)S(1)}, u32[]{:S(2)}, u32[]{:S(2)}) async-start(f32[512,1,384]{2,1,0:T(1,128)} %bitcast.24), calls=%async_computation | async-start | bytes 1572864 | tf_op jit(solution)/shard_map/all_to_all | solution.py:204
  25.4 0.0 copy-start.4
  25.4 0.0 copy-start.5
  25.4 0.7 copy-done.4
  26.1 0.0 copy-done.5
  26.1 0.0 copy-start.1
  26.1 0.0 copy-start.2
  26.1 0.3 side.1
  26.4 26.4 %all-to-all-done = f32[512,1,384]{2,1,0:T(1,128)S(1)} async-done(((f32[512,1,384]{2,1,0:T(1,128)}), f32[512,1,384]{2,1,0:T(1,128)S(1)}, u32[]{:S(2)}, u32[]{:S(2)}) %all-to-all-start) | async-done | bytes 786464 | tf_op jit(solution)/shard_map/all_to_all | solution.py:204
  52.8 0.0 copy-done.3
  52.8 0.0 copy-done.1
  52.8 0.0 copy-done.2
  52.8 5.3 %move.1 = (f32[2048,128]{1,0:T(8,128)}, f32[16,128]{1,0:T(8,128)}, f32[2048,128]{1,0:T(8,128)S(1)}, bf16[2048,256]{1,0:T(8,128)(2,1)S(1)}, f32[1,128]{1,0:T(1,128)S(1)}) custom-call(s32[1]{0:T(128)} %bitcast.core_ref, f32[1536,128]{1,0:T(8,128)S(1)} %bitcast.13, f32[2048,128]{1,0:T(8,128)S(1)} %copy-done.3, f32[2048,128]{1,0:T(8,128)S(1)} %get-tuple-element.14.counts_ref, ...), custom_call_target="tpu_custom_call" | custom-call | flops 4000000000 | bytes 4000000 | tf_op jit(solution)/shard_map/move/pallas_call | solution.py:212
  58.1 3.0 %collective-permute-start = (f32[2048,128]{1,0:T(8,128)S(1)}, f32[2048,128]{1,0:T(8,128)S(1)}, u32[]{:S(2)}, u32[]{:S(2)}) collective-permute-start(f32[2048,128]{1,0:T(8,128)S(1)} %get-tuple-element.20), channel_id=1, source_target_pairs={{0,1},{1,0},{2,3},{3,2},{4,5},{5,4},{6,7},{7,6},{8,9},{9,8},{10,11... | collective-permute-start | bytes 3145736 | tf_op jit(solution)/shard_map/ppermute | solution.py:219
  61.2 2.7 %keep.1 = (f32[2048,128]{1,0:T(8,128)S(1)}, f32[64,128]{1,0:T(8,128)S(1)}, f32[1,64]{1,0:T(1,128)}) custom-call(s32[1]{0:T(128)} %bitcast.core_ref, bf16[2048,256]{1,0:T(8,128)(2,1)S(1)} %get-tuple-element.17.parts_ref, s32[1,2048]{1,0:T(1,128)S(1)} %bitcast.16, s32[1,2048]{1,0:T(1,128)S(1)} %bitcast.19, f32[1,128]{1,0:T(1,128)S(1)} %get-tuple-element.18.hits_ref, ...), custom_call_target="tpu_custom_call" | custom-call | flops 2000000000 | bytes 2000000 | tf_op jit(solution)/shard_map/keep/pallas_call | solution.py:220
  63.9 0.0 collective-permute-done
  63.9 0.1 add.3
  64.0 17.2 %all_to_all.15 = f32[4,512,128]{2,1,0:T(8,128)S(1)} all-to-all(f32[4,512,128]{2,1,0:T(8,128)S(1)} %bitcast.23), channel_id=1, replica_groups={{0,2,4,6},{8,10,12,14},{16,18,20,22},{24,26,28,30},{32,34,36,38},{40,42..., dimensions={0} | all-to-all | bytes 2097152 | tf_op jit(solution)/shard_map/all_to_all | solution.py:233
  81.2 0.1 reduce_sum.9
  81.3 0.0 copy-start
  81.3 13.8 %all_to_all.16.pieces_ref = f32[8,64,128]{2,1,0:T(8,128)S(1)} all-to-all(f32[8,64,128]{2,1,0:T(8,128)S(1)} %bitcast.25), channel_id=1, replica_groups={{0,8,16,24,32,40,48,56},{2,10,18,26,34,42,50,58},{4,12,20,28,36,44,52,6..., dimensions={0} | all-to-all | bytes 524288 | tf_op jit(solution)/shard_map/all_to_all | solution.py:235
  95.0 0.0 copy-done
  95.0 0.6 finish.1
Async XLA Ops:
  3.2 49.6 %copy-start.3 = (f32[2048,128]{1,0:T(8,128)S(1)}, f32[2048,128]{1,0:T(8,128)}, u32[]{:S(2)}) copy-start(f32[2048,128]{1,0:T(8,128)} %cent_ref.1) | copy-start | bytes 3145732
  3.2 49.6 %all-to-all-start = ((f32[512,1,384]{2,1,0:T(1,128)}), f32[512,1,384]{2,1,0:T(1,128)S(1)}, u32[]{:S(2)}, u32[]{:S(2)}) async-start(f32[512,1,384]{2,1,0:T(1,128)} %bitcast.24), calls=%async_computation | async-start | bytes 1572864 | tf_op jit(solution)/shard_map/all_to_all | solution.py:204
  25.4 0.7 copy-start.4
  25.4 0.7 copy-start.5
  26.1 26.7 %copy-start.1 = (s32[2048,1]{0,1:T(1,128)S(1)}, s32[2048,1]{0,1:T(1,128)}, u32[]{:S(2)}) copy-start(s32[2048,1]{0,1:T(1,128)} %param.14) | copy-start | bytes 24580
  26.1 26.7 %copy-start.2 = (s32[2048]{0:T(1024)S(1)}, s32[2048]{0:T(1024)}, u32[]{:S(2)}) copy-start(s32[2048]{0:T(1024)} %param.15) | copy-start | bytes 24580
  58.1 5.8 %collective-permute-start = (f32[2048,128]{1,0:T(8,128)S(1)}, f32[2048,128]{1,0:T(8,128)S(1)}, u32[]{:S(2)}, u32[]{:S(2)}) collective-permute-start(f32[2048,128]{1,0:T(8,128)S(1)} %get-tuple-element.20), channel_id=1, source_target_pairs={{0,1},{1,0},{2,3},{3,2},{4,5},{5,4},{6,7},{7,6},{8,9},{9,8},{10,11... | collective-permute-start | bytes 3145736 | tf_op jit(solution)/shard_map/ppermute | solution.py:219
  81.3 13.8 %copy-start = (f32[64,128]{1,0:T(8,128)S(1)}, f32[64,128]{1,0:T(8,128)}, u32[]{:S(2)}) copy-start(f32[64,128]{1,0:T(8,128)} %upper_ref.1) | copy-start | bytes 98308

commit v5 on v4

--- a/solution.py
+++ b/solution.py
@@ -106,7 +106,7 @@
     first = x * outer + y
     other = low * (inner * outer // fold) + high * inner + x
     mine = jnp.bitwise_and(owner, 1)
-    ids = jnp.where(mine == 0, first, other) * width + sc_ref[...]
+    ids = jnp.where(mine == 1, first, other) * width + sc_ref[...]
     return jnp.where(mine == core, ids, -1)
 
 
@@ -225,10 +225,10 @@
     )(core, parts, oc, sc, hits, upper_counts.reshape(1, width))
     outer, inner, fold = places
     at = lambda y, x, c: (y * inner + x) * 2 + c
-    near = [[at(y, x, 0) for x in range(inner)] for y in range(outer)]
-    near += [[at(h * fold + l, x, 1) for l in range(fold)] for h in range(outer // fold) for x in range(inner)]
-    far = [[at(y, x, 0) for y in range(outer)] for x in range(inner)]
-    far += [[at(h * fold + l, x, 1) for h in range(outer // fold) for x in range(inner)] for l in range(fold)]
+    near = [[at(y, x, 1) for x in range(inner)] for y in range(outer)]
+    near += [[at(h * fold + l, x, 0) for l in range(fold)] for h in range(outer // fold) for x in range(inner)]
+    far = [[at(y, x, 1) for y in range(outer)] for x in range(inner)]
+    far += [[at(h * fold + l, x, 0) for h in range(outer // fold) for x in range(inner)] for l in range(fold)]
     pair = (keep + arrived).reshape(inner, outer * width, LANES)
     merged = jnp.sum(lax.all_to_all(pair, "plane", 0, 0, axis_index_groups=near, tiled=True), axis=0)
     merged = merged.reshape(outer, width, LANES)

time: 96 us -> 96.2 us (level)
  the two profiles are of different devices: /device:TPU:1 before, /device:TPU:64 now
where the time goes in v5:
time: 96.2 us; the launch traced here: 95.9 us
  blocking collectives  33.8 us (35%)
  waiting for transfers between devices  26.2 us (27%)
  starting transfers between devices  22.7 us (24%)
  Pallas kernels  11.6 us (12%)
    all_to_all x1, waiting for transfers between devices, body(): lax.all_to_all(packed.reshape(devices, 1, PARTS * LANES), ('rows', 'plane...  26.2 us
    all_to_all x1, starting transfers between devices, body(): lax.all_to_all(packed.reshape(devices, 1, PARTS * LANES), ('rows', 'plane...  20.7 us
    all_to_all x1, blocking collectives, body(): lax.all_to_all(pair, 'plane', 0, 0, axis_index_groups=near, tiled=True)  18.4 us
    all_to_all x1, blocking collectives, body(): lax.all_to_all(merged, 'plane', 0, 0, axis_index_groups=far, tiled=True)  15.4 us
    pallas_call x1, Pallas kernels, body(): call(functools.partial(move_kernel, width, places), [SMEM] + [VMEM] * 5,...  5.32 us
    pallas_call x1, Pallas kernels, body(): call(functools.partial(keep_kernel, width, places), [SMEM] + [VMEM] * 5,...  2.72 us
    pallas_call x1, Pallas kernels, body(): call(functools.partial(pack_kernel, float(lower)), [ANY] * 5, [((devices...  2.56 us
    ppermute x1, starting transfers between devices, body(): arrived = lax.ppermute(send, 'plane', [(s, s ^ 1) for s in range(shards)])  2.03 us
  transfers between devices with their start and end apart: 2, of which 1 were waited for; matrix products, arithmetic and copies ran while one was open for 0% of the time, Pallas kernels for 3%

profile of v5, /device:TPU:64, one launch (start us, length us, event | category | flops | bytes accessed | tf_op | source)
XLA Modules:
  0.0 95.9 jit_solution(4706470178735429952)
XLA Ops:
  0.6 2.6 %pack.1 = f32[1536,128]{1,0:T(8,128)} custom-call(f32[64,1024]{1,0:T(8,128)} %rows_hbm.1, s32[1,64]{1,0:T(1,128)} %bitcast.26, s32[1,64]{1,0:T(1,128)} %bitcast.27, s32[1,2048]{1,0:T(1,128)} %bitcast.14, s32[1,2048]{1,0:T(1,128)} %bitcast.17), custom_call_target="tpu_custom_call" | custom-call | flops 100000000 | bytes 1000000 | tf_op jit(solution)/shard_map/pack/pallas_call | solution.py:196
  3.2 0.0 copy-start.3
  3.2 20.7 %all-to-all-start = ((f32[512,1,384]{2,1,0:T(1,128)}), f32[512,1,384]{2,1,0:T(1,128)S(1)}, u32[]{:S(2)}, u32[]{:S(2)}) async-start(f32[512,1,384]{2,1,0:T(1,128)} %bitcast.24), calls=%async_computation | async-start | bytes 1572864 | tf_op jit(solution)/shard_map/all_to_all | solution.py:204
  23.9 0.0 copy-start.4
  23.9 0.0 copy-start.5
  24.0 0.7 copy-done.4
  24.6 0.0 copy-done.5
  24.6 0.0 copy-start.1
  24.6 0.0 copy-start.2
  24.6 0.3 side.1
  25.0 26.2 %all-to-all-done = f32[512,1,384]{2,1,0:T(1,128)S(1)} async-done(((f32[512,1,384]{2,1,0:T(1,128)}), f32[512,1,384]{2,1,0:T(1,128)S(1)}, u32[]{:S(2)}, u32[]{:S(2)}) %all-to-all-start) | async-done | bytes 786464 | tf_op jit(solution)/shard_map/all_to_all | solution.py:204
  51.1 0.0 copy-done.3
  51.2 0.0 copy-done.1
  51.2 0.0 copy-done.2
  51.2 5.3 %move.1 = (f32[2048,128]{1,0:T(8,128)}, f32[16,128]{1,0:T(8,128)}, f32[2048,128]{1,0:T(8,128)S(1)}, bf16[2048,256]{1,0:T(8,128)(2,1)S(1)}, f32[1,128]{1,0:T(1,128)S(1)}) custom-call(s32[1]{0:T(128)} %bitcast.core_ref, f32[1536,128]{1,0:T(8,128)S(1)} %bitcast.13, f32[2048,128]{1,0:T(8,128)S(1)} %copy-done.3, f32[2048,128]{1,0:T(8,128)S(1)} %get-tuple-element.14.counts_ref, ...), custom_call_target="tpu_custom_call" | custom-call | flops 4000000000 | bytes 4000000 | tf_op jit(solution)/shard_map/move/pallas_call | solution.py:212
  56.5 2.0 %collective-permute-start = (f32[2048,128]{1,0:T(8,128)S(1)}, f32[2048,128]{1,0:T(8,128)S(1)}, u32[]{:S(2)}, u32[]{:S(2)}) collective-permute-start(f32[2048,128]{1,0:T(8,128)S(1)} %get-tuple-element.20), channel_id=1, source_target_pairs={{0,1},{1,0},{2,3},{3,2},{4,5},{5,4},{6,7},{7,6},{8,9},{9,8},{10,11... | collective-permute-start | bytes 3145736 | tf_op jit(solution)/shard_map/ppermute | solution.py:219
  58.5 2.7 %keep.1 = (f32[2048,128]{1,0:T(8,128)S(1)}, f32[64,128]{1,0:T(8,128)S(1)}, f32[1,64]{1,0:T(1,128)}) custom-call(s32[1]{0:T(128)} %bitcast.core_ref, bf16[2048,256]{1,0:T(8,128)(2,1)S(1)} %get-tuple-element.17.parts_ref, s32[1,2048]{1,0:T(1,128)S(1)} %bitcast.16, s32[1,2048]{1,0:T(1,128)S(1)} %bitcast.19, f32[1,128]{1,0:T(1,128)S(1)} %get-tuple-element.18.hits_ref, ...), custom_call_target="tpu_custom_call" | custom-call | flops 2000000000 | bytes 2000000 | tf_op jit(solution)/shard_map/keep/pallas_call | solution.py:220
  61.2 0.0 collective-permute-done
  61.2 0.1 add.3
  61.4 18.4 %all_to_all.15 = f32[4,512,128]{2,1,0:T(8,128)S(1)} all-to-all(f32[4,512,128]{2,1,0:T(8,128)S(1)} %bitcast.23), channel_id=1, replica_groups={{1,3,5,7},{9,11,13,15},{17,19,21,23},{25,27,29,31},{33,35,37,39},{41,43..., dimensions={0} | all-to-all | bytes 2097152 | tf_op jit(solution)/shard_map/all_to_all | solution.py:233
  79.8 0.1 reduce_sum.9
  79.9 0.0 copy-start
  79.9 15.4 %all_to_all.16.pieces_ref = f32[8,64,128]{2,1,0:T(8,128)S(1)} all-to-all(f32[8,64,128]{2,1,0:T(8,128)S(1)} %bitcast.25), channel_id=1, replica_groups={{1,9,17,25,33,41,49,57},{3,11,19,27,35,43,51,59},{5,13,21,29,37,45,53,6..., dimensions={0} | all-to-all | bytes 524288 | tf_op jit(solution)/shard_map/all_to_all | solution.py:235
  95.2 0.0 copy-done
  95.2 0.6 finish.1
Async XLA Ops:
  3.2 48.0 %copy-start.3 = (f32[2048,128]{1,0:T(8,128)S(1)}, f32[2048,128]{1,0:T(8,128)}, u32[]{:S(2)}) copy-start(f32[2048,128]{1,0:T(8,128)} %cent_ref.1) | copy-start | bytes 3145732
  3.2 47.9 %all-to-all-start = ((f32[512,1,384]{2,1,0:T(1,128)}), f32[512,1,384]{2,1,0:T(1,128)S(1)}, u32[]{:S(2)}, u32[]{:S(2)}) async-start(f32[512,1,384]{2,1,0:T(1,128)} %bitcast.24), calls=%async_computation | async-start | bytes 1572864 | tf_op jit(solution)/shard_map/all_to_all | solution.py:204
  23.9 0.7 copy-start.4
  23.9 0.7 copy-start.5
  24.6 26.5 %copy-start.1 = (s32[2048,1]{0,1:T(1,128)S(1)}, s32[2048,1]{0,1:T(1,128)}, u32[]{:S(2)}) copy-start(s32[2048,1]{0,1:T(1,128)} %param.14) | copy-start | bytes 24580
  24.6 26.5 %copy-start.2 = (s32[2048]{0:T(1024)S(1)}, s32[2048]{0:T(1024)}, u32[]{:S(2)}) copy-start(s32[2048]{0:T(1024)} %param.15) | copy-start | bytes 24580
  56.5 4.8 %collective-permute-start = (f32[2048,128]{1,0:T(8,128)S(1)}, f32[2048,128]{1,0:T(8,128)S(1)}, u32[]{:S(2)}, u32[]{:S(2)}) collective-permute-start(f32[2048,128]{1,0:T(8,128)S(1)} %get-tuple-element.20), channel_id=1, source_target_pairs={{0,1},{1,0},{2,3},{3,2},{4,5},{5,4},{6,7},{7,6},{8,9},{9,8},{10,11... | collective-permute-start | bytes 3145736 | tf_op jit(solution)/shard_map/ppermute | solution.py:219
  79.9 15.4 %copy-start = (f32[64,128]{1,0:T(8,128)S(1)}, f32[64,128]{1,0:T(8,128)}, u32[]{:S(2)}) copy-start(f32[64,128]{1,0:T(8,128)} %upper_ref.1) | copy-start | bytes 98308

commit v6 on v5

--- a/solution.py
+++ b/solution.py
@@ -99,12 +99,12 @@
 
 def ids_of(oc_ref, sc_ref, core, width, places):
     owner = oc_ref[...]
-    outer, inner, fold = places
+    outer, inner = places
     x = jnp.bitwise_and(lax.shift_right_logical(owner, 1), inner - 1)
     y = owner // (2 * inner)
-    low, high = jnp.bitwise_and(y, fold - 1), y // fold
     first = x * outer + y
-    other = low * (inner * outer // fold) + high * inner + x
+    square = jnp.bitwise_and(y, 1) * 2 + jnp.bitwise_and(x, 1)
+    other = square * (inner * outer // 4) + y // 2 * (inner // 2) + x // 2
     mine = jnp.bitwise_and(owner, 1)
     ids = jnp.where(mine == 1, first, other) * width + sc_ref[...]
     return jnp.where(mine == core, ids, -1)
@@ -223,12 +223,14 @@
         [((half, LANES), F32), ((width, LANES), F32), ((1, width), F32)],
         2 * 10**9, 2 * 10**6, "keep",
     )(core, parts, oc, sc, hits, upper_counts.reshape(1, width))
-    outer, inner, fold = places
+    outer, inner = places
     at = lambda y, x, c: (y * inner + x) * 2 + c
+    corners = [(y, x) for y in range(2) for x in range(2)]
+    squares = [(y, x) for y in range(0, outer, 2) for x in range(0, inner, 2)]
     near = [[at(y, x, 1) for x in range(inner)] for y in range(outer)]
-    near += [[at(h * fold + l, x, 0) for l in range(fold)] for h in range(outer // fold) for x in range(inner)]
+    near += [[at(y + v, x + u, 0) for v, u in corners] for y, x in squares]
     far = [[at(y, x, 1) for y in range(outer)] for x in range(inner)]
-    far += [[at(h * fold + l, x, 0) for h in range(outer // fold) for x in range(inner)] for l in range(fold)]
+    far += [[at(y + v, x + u, 0) for y, x in squares] for v, u in corners]
     pair = (keep + arrived).reshape(inner, outer * width, LANES)
     merged = jnp.sum(lax.all_to_all(pair, "plane", 0, 0, axis_index_groups=near, tiled=True), axis=0)
     merged = merged.reshape(outer, width, LANES)
@@ -248,7 +250,7 @@
     everyone = ("rows", "plane")
     inner = inner // 2
     return jax.shard_map(
-        functools.partial(body, (outer, inner, inner)),
+        functools.partial(body, (outer, inner)),
         mesh=fine,
         in_specs=(
             P(everyone, None), P(everyone, None), P(everyone),

time: 96.2 us -> 96.2 us (level)
  the two profiles are of different devices: /device:TPU:64 before, /device:TPU:1 now
where the time goes in v6:
time: 96.2 us; the launch traced here: 95.8 us
  blocking collectives  31.1 us (32%)
  waiting for transfers between devices  26.4 us (27%)
  starting transfers between devices  25.2 us (26%)
  Pallas kernels  11.6 us (12%)
    all_to_all x1, waiting for transfers between devices, body(): lax.all_to_all(packed.reshape(devices, 1, PARTS * LANES), ('rows', 'plane...  26.4 us
    all_to_all x1, starting transfers between devices, body(): lax.all_to_all(packed.reshape(devices, 1, PARTS * LANES), ('rows', 'plane...  22.2 us
    all_to_all x1, blocking collectives, body(): lax.all_to_all(pair, 'plane', 0, 0, axis_index_groups=near, tiled=True)  16.5 us
    all_to_all x1, blocking collectives, body(): lax.all_to_all(merged, 'plane', 0, 0, axis_index_groups=far, tiled=True)  14.6 us
    pallas_call x1, Pallas kernels, body(): call(functools.partial(move_kernel, width, places), [SMEM] + [VMEM] * 5,...  5.32 us
    ppermute x1, starting transfers between devices, body(): arrived = lax.ppermute(send, 'plane', [(s, s ^ 1) for s in range(shards)])  3.02 us
    pallas_call x1, Pallas kernels, body(): call(functools.partial(keep_kernel, width, places), [SMEM] + [VMEM] * 5,...  2.72 us
    pallas_call x1, Pallas kernels, body(): call(functools.partial(pack_kernel, float(lower)), [ANY] * 5, [((devices...  2.56 us
  transfers between devices with their start and end apart: 2, of which 1 were waited for; matrix products, arithmetic and copies ran while one was open for 0% of the time, Pallas kernels for 3%

profile of v6, /device:TPU:1, one launch (start us, length us, event | category | flops | bytes accessed | tf_op | source)
XLA Modules:
  0.0 95.8 jit_solution(2342854976734530237)
XLA Ops:
  0.6 2.6 %pack.1 = f32[1536,128]{1,0:T(8,128)} custom-call(f32[64,1024]{1,0:T(8,128)} %rows_hbm.1, s32[1,64]{1,0:T(1,128)} %bitcast.26, s32[1,64]{1,0:T(1,128)} %bitcast.27, s32[1,2048]{1,0:T(1,128)} %bitcast.14, s32[1,2048]{1,0:T(1,128)} %bitcast.17), custom_call_target="tpu_custom_call" | custom-call | flops 100000000 | bytes 1000000 | tf_op jit(solution)/shard_map/pack/pallas_call | solution.py:196
  3.2 0.0 copy-start.3
  3.2 22.2 %all-to-all-start = ((f32[512,1,384]{2,1,0:T(1,128)}), f32[512,1,384]{2,1,0:T(1,128)S(1)}, u32[]{:S(2)}, u32[]{:S(2)}) async-start(f32[512,1,384]{2,1,0:T(1,128)} %bitcast.24), calls=%async_computation | async-start | bytes 1572864 | tf_op jit(solution)/shard_map/all_to_all | solution.py:204
  25.4 0.0 copy-start.4
  25.4 0.0 copy-start.5
  25.4 0.7 copy-done.4
  26.1 0.0 copy-done.5
  26.1 0.0 copy-start.1
  26.1 0.0 copy-start.2
  26.1 0.3 side.1
  26.4 26.4 %all-to-all-done = f32[512,1,384]{2,1,0:T(1,128)S(1)} async-done(((f32[512,1,384]{2,1,0:T(1,128)}), f32[512,1,384]{2,1,0:T(1,128)S(1)}, u32[]{:S(2)}, u32[]{:S(2)}) %all-to-all-start) | async-done | bytes 786464 | tf_op jit(solution)/shard_map/all_to_all | solution.py:204
  52.8 0.0 copy-done.3
  52.8 0.0 copy-done.1
  52.8 0.0 copy-done.2
  52.8 5.3 %move.1 = (f32[2048,128]{1,0:T(8,128)}, f32[16,128]{1,0:T(8,128)}, f32[2048,128]{1,0:T(8,128)S(1)}, bf16[2048,256]{1,0:T(8,128)(2,1)S(1)}, f32[1,128]{1,0:T(1,128)S(1)}) custom-call(s32[1]{0:T(128)} %bitcast.core_ref, f32[1536,128]{1,0:T(8,128)S(1)} %bitcast.13, f32[2048,128]{1,0:T(8,128)S(1)} %copy-done.3, f32[2048,128]{1,0:T(8,128)S(1)} %get-tuple-element.14.counts_ref, ...), custom_call_target="tpu_custom_call" | custom-call | flops 4000000000 | bytes 4000000 | tf_op jit(solution)/shard_map/move/pallas_call | solution.py:212
  58.1 3.0 %collective-permute-start = (f32[2048,128]{1,0:T(8,128)S(1)}, f32[2048,128]{1,0:T(8,128)S(1)}, u32[]{:S(2)}, u32[]{:S(2)}) collective-permute-start(f32[2048,128]{1,0:T(8,128)S(1)} %get-tuple-element.20), channel_id=1, source_target_pairs={{0,1},{1,0},{2,3},{3,2},{4,5},{5,4},{6,7},{7,6},{8,9},{9,8},{10,11... | collective-permute-start | bytes 3145736 | tf_op jit(solution)/shard_map/ppermute | solution.py:219
  61.2 2.7 %keep.1 = (f32[2048,128]{1,0:T(8,128)S(1)}, f32[64,128]{1,0:T(8,128)S(1)}, f32[1,64]{1,0:T(1,128)}) custom-call(s32[1]{0:T(128)} %bitcast.core_ref, bf16[2048,256]{1,0:T(8,128)(2,1)S(1)} %get-tuple-element.17.parts_ref, s32[1,2048]{1,0:T(1,128)S(1)} %bitcast.16, s32[1,2048]{1,0:T(1,128)S(1)} %bitcast.19, f32[1,128]{1,0:T(1,128)S(1)} %get-tuple-element.18.hits_ref, ...), custom_call_target="tpu_custom_call" | custom-call | flops 2000000000 | bytes 2000000 | tf_op jit(solution)/shard_map/keep/pallas_call | solution.py:220
  63.9 0.0 collective-permute-done
  63.9 0.1 add.3
  64.0 16.5 %all_to_all.15 = f32[4,512,128]{2,1,0:T(8,128)S(1)} all-to-all(f32[4,512,128]{2,1,0:T(8,128)S(1)} %bitcast.23), channel_id=1, replica_groups={{1,3,5,7},{9,11,13,15},{17,19,21,23},{25,27,29,31},{33,35,37,39},{41,43..., dimensions={0} | all-to-all | bytes 2097152 | tf_op jit(solution)/shard_map/all_to_all | solution.py:235
  80.5 0.1 reduce_sum.9
  80.6 0.0 copy-start
  80.6 14.6 %all_to_all.16.pieces_ref = f32[8,64,128]{2,1,0:T(8,128)S(1)} all-to-all(f32[8,64,128]{2,1,0:T(8,128)S(1)} %bitcast.25), channel_id=1, replica_groups={{1,9,17,25,33,41,49,57},{3,11,19,27,35,43,51,59},{5,13,21,29,37,45,53,6..., dimensions={0} | all-to-all | bytes 524288 | tf_op jit(solution)/shard_map/all_to_all | solution.py:237
  95.2 0.0 copy-done
  95.2 0.6 finish.1
Async XLA Ops:
  3.2 49.6 %copy-start.3 = (f32[2048,128]{1,0:T(8,128)S(1)}, f32[2048,128]{1,0:T(8,128)}, u32[]{:S(2)}) copy-start(f32[2048,128]{1,0:T(8,128)} %cent_ref.1) | copy-start | bytes 3145732
  3.2 49.6 %all-to-all-start = ((f32[512,1,384]{2,1,0:T(1,128)}), f32[512,1,384]{2,1,0:T(1,128)S(1)}, u32[]{:S(2)}, u32[]{:S(2)}) async-start(f32[512,1,384]{2,1,0:T(1,128)} %bitcast.24), calls=%async_computation | async-start | bytes 1572864 | tf_op jit(solution)/shard_map/all_to_all | solution.py:204
  25.4 0.7 copy-start.4
  25.4 0.7 copy-start.5
  26.1 26.7 %copy-start.1 = (s32[2048,1]{0,1:T(1,128)S(1)}, s32[2048,1]{0,1:T(1,128)}, u32[]{:S(2)}) copy-start(s32[2048,1]{0,1:T(1,128)} %param.14) | copy-start | bytes 24580
  26.1 26.7 %copy-start.2 = (s32[2048]{0:T(1024)S(1)}, s32[2048]{0:T(1024)}, u32[]{:S(2)}) copy-start(s32[2048]{0:T(1024)} %param.15) | copy-start | bytes 24580
  58.1 5.8 %collective-permute-start = (f32[2048,128]{1,0:T(8,128)S(1)}, f32[2048,128]{1,0:T(8,128)S(1)}, u32[]{:S(2)}, u32[]{:S(2)}) collective-permute-start(f32[2048,128]{1,0:T(8,128)S(1)} %get-tuple-element.20), channel_id=1, source_target_pairs={{0,1},{1,0},{2,3},{3,2},{4,5},{5,4},{6,7},{7,6},{8,9},{9,8},{10,11... | collective-permute-start | bytes 3145736 | tf_op jit(solution)/shard_map/ppermute | solution.py:219
  80.6 14.6 %copy-start = (f32[64,128]{1,0:T(8,128)S(1)}, f32[64,128]{1,0:T(8,128)}, u32[]{:S(2)}) copy-start(f32[64,128]{1,0:T(8,128)} %upper_ref.1) | copy-start | bytes 98308

commit v7 on v6

--- a/solution.py
+++ b/solution.py
@@ -102,12 +102,10 @@
     outer, inner = places
     x = jnp.bitwise_and(lax.shift_right_logical(owner, 1), inner - 1)
     y = owner // (2 * inner)
-    first = x * outer + y
     square = jnp.bitwise_and(y, 1) * 2 + jnp.bitwise_and(x, 1)
-    other = square * (inner * outer // 4) + y // 2 * (inner // 2) + x // 2
+    place = square * (inner * outer // 4) + y // 2 * (inner // 2) + x // 2
     mine = jnp.bitwise_and(owner, 1)
-    ids = jnp.where(mine == 1, first, other) * width + sc_ref[...]
-    return jnp.where(mine == core, ids, -1)
+    return jnp.where(mine == core, place * width + sc_ref[...], -1)
 
 
 def move_kernel(
@@ -227,10 +225,8 @@
     at = lambda y, x, c: (y * inner + x) * 2 + c
     corners = [(y, x) for y in range(2) for x in range(2)]
     squares = [(y, x) for y in range(0, outer, 2) for x in range(0, inner, 2)]
-    near = [[at(y, x, 1) for x in range(inner)] for y in range(outer)]
-    near += [[at(y + v, x + u, 0) for v, u in corners] for y, x in squares]
-    far = [[at(y, x, 1) for y in range(outer)] for x in range(inner)]
-    far += [[at(y + v, x + u, 0) for y, x in squares] for v, u in corners]
+    near = [[at(y + v, x + u, c) for v, u in corners] for y, x in squares for c in range(2)]
+    far = [[at(y + v, x + u, c) for y, x in squares] for v, u in corners for c in range(2)]
     pair = (keep + arrived).reshape(inner, outer * width, LANES)
     merged = jnp.sum(lax.all_to_all(pair, "plane", 0, 0, axis_index_groups=near, tiled=True), axis=0)
     merged = merged.reshape(outer, width, LANES)

time: 96.2 us -> 95.4 us (level); the launches traced: 95.8 us -> 93.8 us
  blocking collectives: 31.1 us -> 29.1 us
    all_to_all x1, blocking collectives: 14.6 us -> 13 us  [body(): lax.all_to_all(merged, 'plane', 0, 0, axis_index_groups=far, tiled=True)]
where the time goes in v7:
time: 95.4 us; the launch traced here: 93.8 us
  blocking collectives  29.1 us (31%)
  waiting for transfers between devices  26.4 us (28%)
  starting transfers between devices  25.2 us (26%)
  Pallas kernels  11.6 us (12%)
    all_to_all x1, waiting for transfers between devices, body(): lax.all_to_all(packed.reshape(devices, 1, PARTS * LANES), ('rows', 'plane...  26.4 us
    all_to_all x1, starting transfers between devices, body(): lax.all_to_all(packed.reshape(devices, 1, PARTS * LANES), ('rows', 'plane...  22.2 us
    all_to_all x1, blocking collectives, body(): lax.all_to_all(pair, 'plane', 0, 0, axis_index_groups=near, tiled=True)  16.1 us
    all_to_all x1, blocking collectives, body(): lax.all_to_all(merged, 'plane', 0, 0, axis_index_groups=far, tiled=True)  13 us
    pallas_call x1, Pallas kernels, body(): call(functools.partial(move_kernel, width, places), [SMEM] + [VMEM] * 5,...  5.32 us
    ppermute x1, starting transfers between devices, body(): arrived = lax.ppermute(send, 'plane', [(s, s ^ 1) for s in range(shards)])  3.02 us
    pallas_call x1, Pallas kernels, body(): call(functools.partial(keep_kernel, width, places), [SMEM] + [VMEM] * 5,...  2.72 us
    pallas_call x1, Pallas kernels, body(): call(functools.partial(pack_kernel, float(lower)), [ANY] * 5, [((devices...  2.56 us
  transfers between devices with their start and end apart: 2, of which 1 were waited for; matrix products, arithmetic and copies ran while one was open for 0% of the time, Pallas kernels for 3%

profile of v7, /device:TPU:1, one launch (start us, length us, event | category | flops | bytes accessed | tf_op | source)
XLA Modules:
  0.0 93.8 jit_solution(15629698250172369877)
XLA Ops:
  0.6 2.6 %pack.1 = f32[1536,128]{1,0:T(8,128)} custom-call(f32[64,1024]{1,0:T(8,128)} %rows_hbm.1, s32[1,64]{1,0:T(1,128)} %bitcast.26, s32[1,64]{1,0:T(1,128)} %bitcast.27, s32[1,2048]{1,0:T(1,128)} %bitcast.14, s32[1,2048]{1,0:T(1,128)} %bitcast.17), custom_call_target="tpu_custom_call" | custom-call | flops 100000000 | bytes 1000000 | tf_op jit(solution)/shard_map/pack/pallas_call | solution.py:194
  3.2 0.0 copy-start.3
  3.2 22.2 %all-to-all-start = ((f32[512,1,384]{2,1,0:T(1,128)}), f32[512,1,384]{2,1,0:T(1,128)S(1)}, u32[]{:S(2)}, u32[]{:S(2)}) async-start(f32[512,1,384]{2,1,0:T(1,128)} %bitcast.24), calls=%async_computation | async-start | bytes 1572864 | tf_op jit(solution)/shard_map/all_to_all | solution.py:202
  25.4 0.0 copy-start.4
  25.4 0.0 copy-start.5
  25.4 0.7 copy-done.4
  26.1 0.0 copy-done.5
  26.1 0.0 copy-start.1
  26.1 0.0 copy-start.2
  26.1 0.3 side.1
  26.4 26.4 %all-to-all-done = f32[512,1,384]{2,1,0:T(1,128)S(1)} async-done(((f32[512,1,384]{2,1,0:T(1,128)}), f32[512,1,384]{2,1,0:T(1,128)S(1)}, u32[]{:S(2)}, u32[]{:S(2)}) %all-to-all-start) | async-done | bytes 786464 | tf_op jit(solution)/shard_map/all_to_all | solution.py:202
  52.8 0.0 copy-done.3
  52.8 0.0 copy-done.1
  52.8 0.0 copy-done.2
  52.8 5.3 %move.1 = (f32[2048,128]{1,0:T(8,128)}, f32[16,128]{1,0:T(8,128)}, f32[2048,128]{1,0:T(8,128)S(1)}, bf16[2048,256]{1,0:T(8,128)(2,1)S(1)}, f32[1,128]{1,0:T(1,128)S(1)}) custom-call(s32[1]{0:T(128)} %bitcast.core_ref, f32[1536,128]{1,0:T(8,128)S(1)} %bitcast.13, f32[2048,128]{1,0:T(8,128)S(1)} %copy-done.3, f32[2048,128]{1,0:T(8,128)S(1)} %get-tuple-element.14.counts_ref, ...), custom_call_target="tpu_custom_call" | custom-call | flops 4000000000 | bytes 4000000 | tf_op jit(solution)/shard_map/move/pallas_call | solution.py:210
  58.1 3.0 %collective-permute-start = (f32[2048,128]{1,0:T(8,128)S(1)}, f32[2048,128]{1,0:T(8,128)S(1)}, u32[]{:S(2)}, u32[]{:S(2)}) collective-permute-start(f32[2048,128]{1,0:T(8,128)S(1)} %get-tuple-element.20), channel_id=1, source_target_pairs={{0,1},{1,0},{2,3},{3,2},{4,5},{5,4},{6,7},{7,6},{8,9},{9,8},{10,11... | collective-permute-start | bytes 3145736 | tf_op jit(solution)/shard_map/ppermute | solution.py:217
  61.2 2.7 %keep.1 = (f32[2048,128]{1,0:T(8,128)S(1)}, f32[64,128]{1,0:T(8,128)S(1)}, f32[1,64]{1,0:T(1,128)}) custom-call(s32[1]{0:T(128)} %bitcast.core_ref, bf16[2048,256]{1,0:T(8,128)(2,1)S(1)} %get-tuple-element.17.parts_ref, s32[1,2048]{1,0:T(1,128)S(1)} %bitcast.16, s32[1,2048]{1,0:T(1,128)S(1)} %bitcast.19, f32[1,128]{1,0:T(1,128)S(1)} %get-tuple-element.18.hits_ref, ...), custom_call_target="tpu_custom_call" | custom-call | flops 2000000000 | bytes 2000000 | tf_op jit(solution)/shard_map/keep/pallas_call | solution.py:218
  63.9 0.0 collective-permute-done
  63.9 0.1 add.3
  64.0 16.1 %all_to_all.15 = f32[4,512,128]{2,1,0:T(8,128)S(1)} all-to-all(f32[4,512,128]{2,1,0:T(8,128)S(1)} %bitcast.23), channel_id=1, replica_groups={{0,2,8,10},{1,3,9,11},{4,6,12,14},{5,7,13,15},{16,18,24,26},{17,19,25,2..., dimensions={0} | all-to-all | bytes 2097152 | tf_op jit(solution)/shard_map/all_to_all | solution.py:231
  80.1 0.1 reduce_sum.9
  80.2 0.0 copy-start
  80.2 13.0 %all_to_all.16.pieces_ref = f32[8,64,128]{2,1,0:T(8,128)S(1)} all-to-all(f32[8,64,128]{2,1,0:T(8,128)S(1)} %bitcast.25), channel_id=1, replica_groups={{0,4,16,20,32,36,48,52},{1,5,17,21,33,37,49,53},{2,6,18,22,34,38,50,54}..., dimensions={0} | all-to-all | bytes 524288 | tf_op jit(solution)/shard_map/all_to_all | solution.py:233
  93.2 0.0 copy-done
  93.2 0.6 finish.1
Async XLA Ops:
  3.2 49.6 %copy-start.3 = (f32[2048,128]{1,0:T(8,128)S(1)}, f32[2048,128]{1,0:T(8,128)}, u32[]{:S(2)}) copy-start(f32[2048,128]{1,0:T(8,128)} %cent_ref.1) | copy-start | bytes 3145732
  3.2 49.6 %all-to-all-start = ((f32[512,1,384]{2,1,0:T(1,128)}), f32[512,1,384]{2,1,0:T(1,128)S(1)}, u32[]{:S(2)}, u32[]{:S(2)}) async-start(f32[512,1,384]{2,1,0:T(1,128)} %bitcast.24), calls=%async_computation | async-start | bytes 1572864 | tf_op jit(solution)/shard_map/all_to_all | solution.py:202
  25.4 0.7 copy-start.4
  25.4 0.7 copy-start.5
  26.1 26.7 %copy-start.1 = (s32[2048,1]{0,1:T(1,128)S(1)}, s32[2048,1]{0,1:T(1,128)}, u32[]{:S(2)}) copy-start(s32[2048,1]{0,1:T(1,128)} %param.14) | copy-start | bytes 24580
  26.1 26.7 %copy-start.2 = (s32[2048]{0:T(1024)S(1)}, s32[2048]{0:T(1024)}, u32[]{:S(2)}) copy-start(s32[2048]{0:T(1024)} %param.15) | copy-start | bytes 24580
  58.1 5.8 %collective-permute-start = (f32[2048,128]{1,0:T(8,128)S(1)}, f32[2048,128]{1,0:T(8,128)S(1)}, u32[]{:S(2)}, u32[]{:S(2)}) collective-permute-start(f32[2048,128]{1,0:T(8,128)S(1)} %get-tuple-element.20), channel_id=1, source_target_pairs={{0,1},{1,0},{2,3},{3,2},{4,5},{5,4},{6,7},{7,6},{8,9},{9,8},{10,11... | collective-permute-start | bytes 3145736 | tf_op jit(solution)/shard_map/ppermute | solution.py:217
  80.2 13.0 %copy-start = (f32[64,128]{1,0:T(8,128)S(1)}, f32[64,128]{1,0:T(8,128)}, u32[]{:S(2)}) copy-start(f32[64,128]{1,0:T(8,128)} %upper_ref.1) | copy-start | bytes 98308

commit v8 on v3

--- a/solution.py
+++ b/solution.py
@@ -109,14 +109,18 @@
         out_ref[at : at + BLOCK, :] = both[:, :LANES] + both[:, LANES:]
 
 
-def ids_of(oc_ref, sc_ref, core, width):
+def ids_of(oc_ref, sc_ref, core, width, places):
     owner = oc_ref[...]
-    ids = lax.shift_right_logical(owner, 1) * width + sc_ref[...]
-    return jnp.where(jnp.bitwise_and(owner, 1) == core, ids, -1)
+    outer, inner = places
+    x = jnp.bitwise_and(lax.shift_right_logical(owner, 1), inner - 1)
+    y = owner // (2 * inner)
+    square = jnp.bitwise_and(y, 1) * 2 + jnp.bitwise_and(x, 1)
+    place = square * (inner * outer // 4) + y // 2 * (inner // 2) + x // 2
+    return jnp.where(jnp.bitwise_and(owner, 1) == core, place * width + sc_ref[...], -1)
 
 
 def move_kernel(
-    width, pairs, core_ref, got_ref, cent_ref, counts_ref, oc_ref, sc_ref,
+    width, pairs, places, core_ref, got_ref, cent_ref, counts_ref, oc_ref, sc_ref,
     moved_hbm, new_counts_ref, send_ref, parts_ref, hits_ref, moved_ref, sem,
 ):
     sources = got_ref.shape[0] // PARTS
@@ -151,17 +155,17 @@
             new_counts_ref[row : row + 1, :] = jnp.sum(block, axis=0, keepdims=True)
     copy = pltpu.make_async_copy(moved_ref, moved_hbm, sem)
     copy.start()
-    partial_sums(ids_of(oc_ref, sc_ref, 1 - core_ref[0], width), parts_ref, send_ref)
+    partial_sums(ids_of(oc_ref, sc_ref, 1 - core_ref[0], width, places), parts_ref, send_ref)
     copy.wait()
 
 
 def keep_kernel(
-    width, core_ref, parts_ref, oc_ref, sc_ref, hits_ref, upper_counts_ref, keep_ref, members_ref, new_counts_ref,
+    width, places, core_ref, parts_ref, oc_ref, sc_ref, hits_ref, upper_counts_ref, keep_ref, members_ref, new_counts_ref,
 ):
     hits = hits_ref[...]
     members_ref[...] = columns(hits)[LANES - width :]
     new_counts_ref[...] = upper_counts_ref[...] + hits[:, LANES - width :]
-    partial_sums(ids_of(oc_ref, sc_ref, core_ref[0], width), parts_ref, keep_ref)
+    partial_sums(ids_of(oc_ref, sc_ref, core_ref[0], width, places), parts_ref, keep_ref)
 
 
 def finish_kernel(pieces_ref, upper_ref, members_ref, counts_ref, out_ref):
@@ -189,9 +193,11 @@
 
 
 def body(rows_data, owner_rows, slot_rows, centroids, counts, owner_cent, slot_cent, upper, upper_counts):
-    exchange = ("core", "rows", "cx", "x")
+    exchange = ("core", "rows", "yh", "yl", "xh", "xl")
+    corner, square = ("yl", "xl"), ("yh", "xh")
+    places = tuple(lax.axis_size(axes) for axes in (("yh", "yl"), ("xh", "xl")))
     groups = lax.axis_size("rows")
-    shards = lax.axis_size(("cx", "x", "core"))
+    shards = lax.axis_size(("yh", "yl", "xh", "xl", "core"))
     pairs = shards // 2
     devices = groups * shards
     batch, features = rows_data.shape
@@ -219,7 +225,7 @@
         10**7, 10**6, "side",
     )(counts.reshape(lower // LANES, LANES), upper_counts.reshape(1, width))
     moved, new_counts, send, parts, hits = call(
-        functools.partial(move_kernel, width, pairs),
+        functools.partial(move_kernel, width, pairs, places),
         [SMEM] + [VMEM] * 5,
         [((lower, LANES), F32), ((lower // LANES, LANES), F32), ((half, LANES), F32), ((lower, 2 * LANES), BF16), ((1, LANES), F32)],
         4 * 10**9, 4 * 10**6, "move", [ANY] + [VMEM] * 4,
@@ -227,13 +233,14 @@
     )(core, got, centroids, wide_counts, oc, sc)
     arrived = lax.ppermute(send, "core", [(0, 1), (1, 0)])
     keep, members, new_upper_counts = call(
-        functools.partial(keep_kernel, width),
+        functools.partial(keep_kernel, width, places),
         [SMEM] + [VMEM] * 5,
         [((half, LANES), F32), ((width, LANES), F32), ((1, width), F32)],
         2 * 10**9, 2 * 10**6, "keep",
     )(core, parts, oc, sc, hits, upper_counts.reshape(1, width))
-    pair = (keep + arrived).reshape(pairs, width, LANES)
-    pieces = lax.all_to_all(pair, ("cx", "x"), 0, 0, tiled=True)
+    pair = (keep + arrived).reshape(4, half // 4, LANES)
+    merged = jnp.sum(lax.all_to_all(pair, corner, 0, 0, tiled=True), axis=0)
+    pieces = lax.all_to_all(merged.reshape(pairs // 4, width, LANES), square, 0, 0, tiled=True)
     (new_upper,) = call(
         finish_kernel,
         [VMEM] * 4,
@@ -245,9 +252,10 @@
 
 def solution(mesh):
     groups, outer, inner = mesh.devices.shape
-    fine = Mesh(mesh.devices.reshape(groups, outer, inner // 2, 2), ("rows", "cx", "x", "core"))
-    everyone = ("rows", "cx", "x", "core")
-    plane = ("cx", "x", "core")
+    shape = (groups, outer // 2, 2, inner // 4, 2, 2)
+    fine = Mesh(mesh.devices.reshape(shape), ("rows", "yh", "yl", "xh", "xl", "core"))
+    plane = ("yh", "yl", "xh", "xl", "core")
+    everyone = ("rows", *plane)
     return jax.shard_map(
         body,
         mesh=fine,

time: 96 us -> 95.4 us (level)
  blocking collectives: 31.3 us -> 29.9 us
    all_to_all x1 -> x2, blocking collectives: 31.3 us -> 29.9 us  [the longest x1 16 us: body(): merged = jnp.sum(lax.all_to_all(pair, corner, 0, 0, tiled=True), axis=0)]
where the time goes in v8:
time: 95.4 us; the launch traced here: 93.8 us
  blocking collectives  29.9 us (31%)
  waiting for transfers between devices  26.2 us (27%)
  starting transfers between devices  24.5 us (26%)
  Pallas kernels  11.6 us (12%)
    all_to_all x1, waiting for transfers between devices, body(): lax.all_to_all(packed.reshape(devices, 1, PARTS * LANES), exchange, 0, 0,...  26.2 us
    all_to_all x1, starting transfers between devices, body(): lax.all_to_all(packed.reshape(devices, 1, PARTS * LANES), exchange, 0, 0,...  22.2 us
    all_to_all x1, blocking collectives, body(): merged = jnp.sum(lax.all_to_all(pair, corner, 0, 0, tiled=True), axis=0)  16 us
    all_to_all x1, blocking collectives, body(): lax.all_to_all(merged.reshape(pairs // 4, width, LANES), square, 0, 0, ti...  13.9 us
    pallas_call x1, Pallas kernels, body(): call(functools.partial(move_kernel, width, pairs, places), [SMEM] + [VMEM...  5.32 us
    pallas_call x1, Pallas kernels, body(): call(functools.partial(keep_kernel, width, places), [SMEM] + [VMEM] * 5,...  2.72 us
    pallas_call x1, Pallas kernels, body(): call(functools.partial(pack_kernel, float(lower)), [ANY] * 5, [((devices...  2.56 us
    ppermute x1, starting transfers between devices, body(): arrived = lax.ppermute(send, 'core', [(0, 1), (1, 0)])  2.28 us
  transfers between devices with their start and end apart: 2, of which 1 were waited for; matrix products, arithmetic and copies ran while one was open for 0% of the time, Pallas kernels for 3%

profile of v8, /device:TPU:1, one launch (start us, length us, event | category | flops | bytes accessed | tf_op | source)
XLA Modules:
  0.0 93.8 jit_solution(17996054305069829754)
XLA Ops:
  0.6 2.6 %pack.1 = f32[1536,128]{1,0:T(8,128)} custom-call(f32[64,1024]{1,0:T(8,128)} %rows_hbm.1, s32[1,64]{1,0:T(1,128)} %bitcast.26, s32[1,64]{1,0:T(1,128)} %bitcast.27, s32[1,2048]{1,0:T(1,128)} %bitcast.14, s32[1,2048]{1,0:T(1,128)} %bitcast.17), custom_call_target="tpu_custom_call" | custom-call | flops 100000000 | bytes 1000000 | tf_op jit(solution)/shard_map/pack/pallas_call | solution.py:211
  3.2 0.0 copy-start.3
  3.2 22.2 %all-to-all-start = ((f32[512,1,384]{2,1,0:T(1,128)}), f32[512,1,384]{2,1,0:T(1,128)S(1)}, u32[]{:S(2)}, u32[]{:S(2)}) async-start(f32[512,1,384]{2,1,0:T(1,128)} %bitcast.24), calls=%async_computation | async-start | bytes 1572864 | tf_op jit(solution)/shard_map/all_to_all | solution.py:219
  25.4 0.0 copy-start.4
  25.4 0.0 copy-start.5
  25.4 0.7 copy-done.4
  26.1 0.0 copy-done.5
  26.1 0.0 copy-start.1
  26.1 0.0 copy-start.2
  26.1 0.3 side.1
  26.4 26.2 %all-to-all-done = f32[512,1,384]{2,1,0:T(1,128)S(1)} async-done(((f32[512,1,384]{2,1,0:T(1,128)}), f32[512,1,384]{2,1,0:T(1,128)S(1)}, u32[]{:S(2)}, u32[]{:S(2)}) %all-to-all-start) | async-done | bytes 786464 | tf_op jit(solution)/shard_map/all_to_all | solution.py:219
  52.6 0.0 copy-done.3
  52.6 0.0 copy-done.1
  52.6 0.0 copy-done.2
  52.6 5.3 %move.1 = (f32[2048,128]{1,0:T(8,128)}, f32[16,128]{1,0:T(8,128)}, f32[2048,128]{1,0:T(8,128)S(1)}, bf16[2048,256]{1,0:T(8,128)(2,1)S(1)}, f32[1,128]{1,0:T(1,128)S(1)}) custom-call(s32[1]{0:T(128)} %bitcast.core_ref, f32[1536,128]{1,0:T(8,128)S(1)} %bitcast.13, f32[2048,128]{1,0:T(8,128)S(1)} %copy-done.3, f32[2048,128]{1,0:T(8,128)S(1)} %get-tuple-element.14.counts_ref, ...), custom_call_target="tpu_custom_call" | custom-call | flops 4000000000 | bytes 4000000 | tf_op jit(solution)/shard_map/move/pallas_call | solution.py:227
  58.0 2.3 %collective-permute-start = (f32[2048,128]{1,0:T(8,128)S(1)}, f32[2048,128]{1,0:T(8,128)S(1)}, u32[]{:S(2)}, u32[]{:S(2)}) collective-permute-start(f32[2048,128]{1,0:T(8,128)S(1)} %get-tuple-element.20), channel_id=1, source_target_pairs={{0,1},{1,0},{2,3},{3,2},{4,5},{5,4},{6,7},{7,6},{8,9},{9,8},{10,11... | collective-permute-start | bytes 3145736 | tf_op jit(solution)/shard_map/ppermute | solution.py:234
  60.3 2.7 %keep.1 = (f32[2048,128]{1,0:T(8,128)S(1)}, f32[64,128]{1,0:T(8,128)S(1)}, f32[1,64]{1,0:T(1,128)}) custom-call(s32[1]{0:T(128)} %bitcast.core_ref, bf16[2048,256]{1,0:T(8,128)(2,1)S(1)} %get-tuple-element.17.parts_ref, s32[1,2048]{1,0:T(1,128)S(1)} %bitcast.16, s32[1,2048]{1,0:T(1,128)S(1)} %bitcast.19, f32[1,128]{1,0:T(1,128)S(1)} %get-tuple-element.18.hits_ref, ...), custom_call_target="tpu_custom_call" | custom-call | flops 2000000000 | bytes 2000000 | tf_op jit(solution)/shard_map/keep/pallas_call | solution.py:235
  63.0 0.0 collective-permute-done
  63.0 0.2 add.3
  63.1 16.0 %all_to_all.15 = f32[4,512,128]{2,1,0:T(8,128)S(1)} all-to-all(f32[4,512,128]{2,1,0:T(8,128)S(1)} %bitcast.23), channel_id=1, replica_groups=mesh['rows'=8,'yh'=4,'yl'=2,'xh'=2,'xl'=2,'core'=2] {'yl','xl'}, dimensions={0} | all-to-all | bytes 2097152 | tf_op jit(solution)/shard_map/all_to_all | solution.py:242
  79.2 0.1 reduce_sum.9
  79.2 0.0 copy-start
  79.2 13.9 %all_to_all.16.pieces_ref = f32[8,64,128]{2,1,0:T(8,128)S(1)} all-to-all(f32[8,64,128]{2,1,0:T(8,128)S(1)} %bitcast.25), channel_id=1, replica_groups=mesh['rows'=8,'yh'=4,'yl'=2,'xh'=2,'xl'=2,'core'=2] {'yh','xh'}, dimensions={0} | all-to-all | bytes 524288 | tf_op jit(solution)/shard_map/all_to_all | solution.py:243
  93.2 0.0 copy-done
  93.2 0.6 finish.1
Async XLA Ops:
  3.2 49.4 %copy-start.3 = (f32[2048,128]{1,0:T(8,128)S(1)}, f32[2048,128]{1,0:T(8,128)}, u32[]{:S(2)}) copy-start(f32[2048,128]{1,0:T(8,128)} %cent_ref.1) | copy-start | bytes 3145732
  3.2 49.4 %all-to-all-start = ((f32[512,1,384]{2,1,0:T(1,128)}), f32[512,1,384]{2,1,0:T(1,128)S(1)}, u32[]{:S(2)}, u32[]{:S(2)}) async-start(f32[512,1,384]{2,1,0:T(1,128)} %bitcast.24), calls=%async_computation | async-start | bytes 1572864 | tf_op jit(solution)/shard_map/all_to_all | solution.py:219
  25.4 0.7 copy-start.4
  25.4 0.7 copy-start.5
  26.1 26.5 %copy-start.1 = (s32[2048,1]{0,1:T(1,128)S(1)}, s32[2048,1]{0,1:T(1,128)}, u32[]{:S(2)}) copy-start(s32[2048,1]{0,1:T(1,128)} %param.14) | copy-start | bytes 24580
  26.1 26.5 %copy-start.2 = (s32[2048]{0:T(1024)S(1)}, s32[2048]{0:T(1024)}, u32[]{:S(2)}) copy-start(s32[2048]{0:T(1024)} %param.15) | copy-start | bytes 24580
  58.0 5.0 %collective-permute-start = (f32[2048,128]{1,0:T(8,128)S(1)}, f32[2048,128]{1,0:T(8,128)S(1)}, u32[]{:S(2)}, u32[]{:S(2)}) collective-permute-start(f32[2048,128]{1,0:T(8,128)S(1)} %get-tuple-element.20), channel_id=1, source_target_pairs={{0,1},{1,0},{2,3},{3,2},{4,5},{5,4},{6,7},{7,6},{8,9},{9,8},{10,11... | collective-permute-start | bytes 3145736 | tf_op jit(solution)/shard_map/ppermute | solution.py:234
  79.2 13.9 %copy-start = (f32[64,128]{1,0:T(8,128)S(1)}, f32[64,128]{1,0:T(8,128)}, u32[]{:S(2)}) copy-start(f32[64,128]{1,0:T(8,128)} %upper_ref.1) | copy-start | bytes 98308

commit v9 on v8

--- a/solution.py
+++ b/solution.py
@@ -114,8 +114,8 @@
     outer, inner = places
     x = jnp.bitwise_and(lax.shift_right_logical(owner, 1), inner - 1)
     y = owner // (2 * inner)
-    square = jnp.bitwise_and(y, 1) * 2 + jnp.bitwise_and(x, 1)
-    place = square * (inner * outer // 4) + y // 2 * (inner // 2) + x // 2
+    square = jnp.bitwise_and(x, 1) * 2 + jnp.bitwise_and(y, 1)
+    place = square * (inner * outer // 4) + x // 2 * (outer // 2) + y // 2
     return jnp.where(jnp.bitwise_and(owner, 1) == core, place * width + sc_ref[...], -1)
 
 
@@ -194,7 +194,7 @@
 
 def body(rows_data, owner_rows, slot_rows, centroids, counts, owner_cent, slot_cent, upper, upper_counts):
     exchange = ("core", "rows", "yh", "yl", "xh", "xl")
-    corner, square = ("yl", "xl"), ("yh", "xh")
+    corner, square = ("xl", "yl"), ("xh", "yh")
     places = tuple(lax.axis_size(axes) for axes in (("yh", "yl"), ("xh", "xl")))
     groups = lax.axis_size("rows")
     shards = lax.axis_size(("yh", "yl", "xh", "xl", "core"))

time: 95.4 us -> 97.2 us (1.019)
  the two profiles are of different devices: /device:TPU:1 before, /device:TPU:8 now
where the time goes in v9:
time: 97.2 us; the launch traced here: 96.9 us
  blocking collectives  35 us (36%)
  waiting for transfers between devices  25.4 us (26%)
  starting transfers between devices  23.2 us (24%)
  Pallas kernels  11.6 us (12%)
    all_to_all x1, waiting for transfers between devices, body(): lax.all_to_all(packed.reshape(devices, 1, PARTS * LANES), exchange, 0, 0,...  25.4 us
    all_to_all x1, starting transfers between devices, body(): lax.all_to_all(packed.reshape(devices, 1, PARTS * LANES), exchange, 0, 0,...  21.1 us
    all_to_all x1, blocking collectives, body(): lax.all_to_all(merged.reshape(pairs // 4, width, LANES), square, 0, 0, ti...  17.7 us
    all_to_all x1, blocking collectives, body(): merged = jnp.sum(lax.all_to_all(pair, corner, 0, 0, tiled=True), axis=0)  17.4 us
    pallas_call x1, Pallas kernels, body(): call(functools.partial(move_kernel, width, pairs, places), [SMEM] + [VMEM...  5.32 us
    pallas_call x1, Pallas kernels, body(): call(functools.partial(keep_kernel, width, places), [SMEM] + [VMEM] * 5,...  2.72 us
    pallas_call x1, Pallas kernels, body(): call(functools.partial(pack_kernel, float(lower)), [ANY] * 5, [((devices...  2.56 us
    ppermute x1, starting transfers between devices, body(): arrived = lax.ppermute(send, 'core', [(0, 1), (1, 0)])  2.11 us
  transfers between devices with their start and end apart: 2, of which 1 were waited for; matrix products, arithmetic and copies ran while one was open for 0% of the time, Pallas kernels for 3%

profile of v9, /device:TPU:8, one launch (start us, length us, event | category | flops | bytes accessed | tf_op | source)
XLA Modules:
  0.0 96.9 jit_solution(11135924440706097714)
XLA Ops:
  0.6 2.6 %pack.1 = f32[1536,128]{1,0:T(8,128)} custom-call(f32[64,1024]{1,0:T(8,128)} %rows_hbm.1, s32[1,64]{1,0:T(1,128)} %bitcast.26, s32[1,64]{1,0:T(1,128)} %bitcast.27, s32[1,2048]{1,0:T(1,128)} %bitcast.14, s32[1,2048]{1,0:T(1,128)} %bitcast.17), custom_call_target="tpu_custom_call" | custom-call | flops 100000000 | bytes 1000000 | tf_op jit(solution)/shard_map/pack/pallas_call | solution.py:211
  3.2 0.0 copy-start.3
  3.2 21.1 %all-to-all-start = ((f32[512,1,384]{2,1,0:T(1,128)}), f32[512,1,384]{2,1,0:T(1,128)S(1)}, u32[]{:S(2)}, u32[]{:S(2)}) async-start(f32[512,1,384]{2,1,0:T(1,128)} %bitcast.24), calls=%async_computation | async-start | bytes 1572864 | tf_op jit(solution)/shard_map/all_to_all | solution.py:219
  24.3 0.0 copy-start.4
  24.4 0.0 copy-start.5
  24.4 0.7 copy-done.4
  25.0 0.0 copy-done.5
  25.0 0.0 copy-start.1
  25.0 0.0 copy-start.2
  25.0 0.3 side.1
  25.4 25.4 %all-to-all-done = f32[512,1,384]{2,1,0:T(1,128)S(1)} async-done(((f32[512,1,384]{2,1,0:T(1,128)}), f32[512,1,384]{2,1,0:T(1,128)S(1)}, u32[]{:S(2)}, u32[]{:S(2)}) %all-to-all-start) | async-done | bytes 786464 | tf_op jit(solution)/shard_map/all_to_all | solution.py:219
  50.8 0.0 copy-done.3
  50.8 0.0 copy-done.1
  50.8 0.0 copy-done.2
  50.8 5.3 %move.1 = (f32[2048,128]{1,0:T(8,128)}, f32[16,128]{1,0:T(8,128)}, f32[2048,128]{1,0:T(8,128)S(1)}, bf16[2048,256]{1,0:T(8,128)(2,1)S(1)}, f32[1,128]{1,0:T(1,128)S(1)}) custom-call(s32[1]{0:T(128)} %bitcast.core_ref, f32[1536,128]{1,0:T(8,128)S(1)} %bitcast.13, f32[2048,128]{1,0:T(8,128)S(1)} %copy-done.3, f32[2048,128]{1,0:T(8,128)S(1)} %get-tuple-element.14.counts_ref, ...), custom_call_target="tpu_custom_call" | custom-call | flops 4000000000 | bytes 4000000 | tf_op jit(solution)/shard_map/move/pallas_call | solution.py:227
  56.1 2.1 %collective-permute-start = (f32[2048,128]{1,0:T(8,128)S(1)}, f32[2048,128]{1,0:T(8,128)S(1)}, u32[]{:S(2)}, u32[]{:S(2)}) collective-permute-start(f32[2048,128]{1,0:T(8,128)S(1)} %get-tuple-element.20), channel_id=1, source_target_pairs={{0,1},{1,0},{2,3},{3,2},{4,5},{5,4},{6,7},{7,6},{8,9},{9,8},{10,11... | collective-permute-start | bytes 3145736 | tf_op jit(solution)/shard_map/ppermute | solution.py:234
  58.2 2.7 %keep.1 = (f32[2048,128]{1,0:T(8,128)S(1)}, f32[64,128]{1,0:T(8,128)S(1)}, f32[1,64]{1,0:T(1,128)}) custom-call(s32[1]{0:T(128)} %bitcast.core_ref, bf16[2048,256]{1,0:T(8,128)(2,1)S(1)} %get-tuple-element.17.parts_ref, s32[1,2048]{1,0:T(1,128)S(1)} %bitcast.16, s32[1,2048]{1,0:T(1,128)S(1)} %bitcast.19, f32[1,128]{1,0:T(1,128)S(1)} %get-tuple-element.18.hits_ref, ...), custom_call_target="tpu_custom_call" | custom-call | flops 2000000000 | bytes 2000000 | tf_op jit(solution)/shard_map/keep/pallas_call | solution.py:235
  61.0 0.0 collective-permute-done
  61.0 0.2 add.3
  61.1 17.4 %all_to_all.15 = f32[4,512,128]{2,1,0:T(8,128)S(1)} all-to-all(f32[4,512,128]{2,1,0:T(8,128)S(1)} %bitcast.23), channel_id=1, replica_groups=mesh['rows'=8,'yh'=4,'yl'=2,'xh'=2,'xl'=2,'core'=2] {'xl','yl'}, dimensions={0} | all-to-all | bytes 2097152 | tf_op jit(solution)/shard_map/all_to_all | solution.py:242
  78.5 0.1 reduce_sum.9
  78.6 0.0 copy-start
  78.6 17.7 %all_to_all.16.pieces_ref = f32[8,64,128]{2,1,0:T(8,128)S(1)} all-to-all(f32[8,64,128]{2,1,0:T(8,128)S(1)} %bitcast.25), channel_id=1, replica_groups=mesh['rows'=8,'yh'=4,'yl'=2,'xh'=2,'xl'=2,'core'=2] {'xh','yh'}, dimensions={0} | all-to-all | bytes 524288 | tf_op jit(solution)/shard_map/all_to_all | solution.py:243
  96.2 0.0 copy-done
  96.2 0.6 finish.1
Async XLA Ops:
  3.2 47.6 %copy-start.3 = (f32[2048,128]{1,0:T(8,128)S(1)}, f32[2048,128]{1,0:T(8,128)}, u32[]{:S(2)}) copy-start(f32[2048,128]{1,0:T(8,128)} %cent_ref.1) | copy-start | bytes 3145732
  3.2 47.6 %all-to-all-start = ((f32[512,1,384]{2,1,0:T(1,128)}), f32[512,1,384]{2,1,0:T(1,128)S(1)}, u32[]{:S(2)}, u32[]{:S(2)}) async-start(f32[512,1,384]{2,1,0:T(1,128)} %bitcast.24), calls=%async_computation | async-start | bytes 1572864 | tf_op jit(solution)/shard_map/all_to_all | solution.py:219
  24.3 0.7 copy-start.4
  24.4 0.7 copy-start.5
  25.0 25.8 %copy-start.1 = (s32[2048,1]{0,1:T(1,128)S(1)}, s32[2048,1]{0,1:T(1,128)}, u32[]{:S(2)}) copy-start(s32[2048,1]{0,1:T(1,128)} %param.14) | copy-start | bytes 24580
  25.0 25.8 %copy-start.2 = (s32[2048]{0:T(1024)S(1)}, s32[2048]{0:T(1024)}, u32[]{:S(2)}) copy-start(s32[2048]{0:T(1024)} %param.15) | copy-start | bytes 24580
  56.1 4.8 %collective-permute-start = (f32[2048,128]{1,0:T(8,128)S(1)}, f32[2048,128]{1,0:T(8,128)S(1)}, u32[]{:S(2)}, u32[]{:S(2)}) collective-permute-start(f32[2048,128]{1,0:T(8,128)S(1)} %get-tuple-element.20), channel_id=1, source_target_pairs={{0,1},{1,0},{2,3},{3,2},{4,5},{5,4},{6,7},{7,6},{8,9},{9,8},{10,11... | collective-permute-start | bytes 3145736 | tf_op jit(solution)/shard_map/ppermute | solution.py:234
  78.6 17.7 %copy-start = (f32[64,128]{1,0:T(8,128)S(1)}, f32[64,128]{1,0:T(8,128)}, u32[]{:S(2)}) copy-start(f32[64,128]{1,0:T(8,128)} %upper_ref.1) | copy-start | bytes 98308
